TPU v7x, 32 devices: a whole 2x2x4 slice. The times are simulated.
32 devices in a mesh: tm: 8 (over z, x), chan: 4 (over y, core).
Axes of the slice: x: 2, y: 2, z: 4, core: 2. Of those that a mesh axis runs over, the one named last changes fastest.
Arguments:
- samples: bfloat16 [4096, 16384], P('tm', 'chan'), may hold values from -180 to 180
- sketch: bfloat16 [16384, 512], P('chan'), may hold values from -0.046875 to 0.046875
Outputs:
- coords: float32 [4096, 512], P('tm')
- weights: float32 [4096], P('tm')
All inputs are finite; a program needn't handle non-finite values.
Results may differ from a plain program's by a relative error of at most 0.0033.
Values may be sent and summed in bfloat16 or wider, within the bound.
A program may use at most 64 MiB of HBM per device.

v0:
```python
import jax
import jax.numpy as jnp
from jax import lax
from jax.sharding import PartitionSpec as P

C = 16384
ROUNDS = 2


def shards(samples, sketch):
    sketched = lax.psum(jnp.dot(samples, sketch, preferred_element_type=jnp.float32), "chan")
    weights = jnp.ones((samples.shape[0],), jnp.float32)
    coords = jnp.zeros(sketched.shape, jnp.float32)
    for step in range(ROUNDS):
        weighted = ((weights * weights)[:, None] * sketched).astype(jnp.bfloat16)
        local_factor = jnp.einsum(
            "sc,sk->ck", samples, weighted, preferred_element_type=jnp.float32
        )
        factor = lax.psum(local_factor, "tm")
        local_gram = jnp.dot(
            factor.T, factor, precision=lax.Precision.HIGHEST, preferred_element_type=jnp.float32
        )
        gram = lax.psum(local_gram, "chan")
        lower = jnp.linalg.cholesky(gram)
        basis = lax.linalg.triangular_solve(
            lower, factor, left_side=False, lower=True, transpose_a=True
        ).astype(jnp.bfloat16)
        local_coords = jnp.dot(samples, basis, preferred_element_type=jnp.float32)
        coords = lax.psum(local_coords, "chan")
        back = jnp.einsum(
            "sk,ck->sc", coords.astype(jnp.bfloat16), basis, preferred_element_type=jnp.float32
        )
        resid = samples.astype(jnp.float32) - back
        energy = lax.psum(jnp.sum(resid * resid, axis=1), "chan")
        weights = jnp.minimum(1.0, 3.0 / jnp.sqrt(energy / C + 1e-06))
    return (coords, weights)


def solution(mesh):
    in_specs = (P("tm", "chan"), P("chan", None))
    out_specs = (P("tm", None), P("tm"))
    return jax.shard_map(shards, mesh=mesh, in_specs=in_specs, out_specs=out_specs, check_vma=False)
```

profile of v0, /device:TPU:29, one launch (start us, length us, event | category | flops | bytes accessed | tf_op | source)
XLA Modules:
  0.0 1134.6 jit_solution(4831139212829809344)
XLA Ops:
  7.2 6.8 fusion.86
  14.0 36.5 %all-reduce.9.cloned.1.call-done = f32[512,512]{1,0:T(8,128)} async-done(((f32[512,512]{1,0:T(8,128)}), f32[512,512]{1,0:T(8,128)}) %all-reduce.9.cloned.1.call-update) | async-done | bytes 1048592 | tf_op jit(solution)/shard_map/psum | solution.py:11
  50.5 8.1 convolution_bitcast_fusion.1
  58.7 269.4 %all-reduce.11.cloned.1.call-done = f32[4096,512]{0,1:T(8,128)} async-done(((f32[4096,512]{0,1:T(8,128)}), f32[4096,512]{0,1:T(8,128)}) %all-reduce.11.cloned.1.call-update) | async-done | bytes 8388624 | tf_op jit(solution)/shard_map/psum | solution.py:19
  328.1 17.2 %fusion.87 = f32[512,512]{0,1:T(8,128)} fusion(f32[4096,512]{0,1:T(8,128)} %all-reduce.11.cloned.1.call-done), kind=kOutput, calls=%fused_computation.154 | convolution fusion | flops 12884901888 | bytes 9437184 | tf_op jit(solution)/shard_map/dot_general | solution.py:20
  345.6 36.6 %all-reduce.13.cloned.1.call-done = f32[512,512]{0,1:T(8,128)} async-done(((f32[512,512]{0,1:T(8,128)}), f32[512,512]{0,1:T(8,128)}) %all-reduce.13.cloned.1.call-update) | async-done | bytes 1048592 | tf_op jit(solution)/shard_map/psum | solution.py:23
  385.2 11.7 %cholesky.286 = f32[128,128]{1,0:T(8,128)S(1)} custom-call(f32[128,128]{1,0:T(8,128)S(1)} %cholesky.426), custom_call_target="Cholesky" | custom-call | tf_op jit(solution)/shard_map/jit(cholesky)/cholesky | solution.py:24
  396.9 9.8 custom-call.27
  407.5 11.7 %cholesky.305 = f32[128,128]{1,0:T(8,128)S(1)} custom-call(f32[128,128]{1,0:T(8,128)S(1)} %cholesky.430), custom_call_target="Cholesky" | custom-call | tf_op jit(solution)/shard_map/jit(cholesky)/cholesky | solution.py:24
  419.3 10.2 custom-call.28
  430.1 11.7 %cholesky.326 = f32[128,128]{1,0:T(8,128)S(1)} custom-call(f32[128,128]{1,0:T(8,128)S(1)} %cholesky.435), custom_call_target="Cholesky" | custom-call | tf_op jit(solution)/shard_map/jit(cholesky)/cholesky | solution.py:24
  442.5 9.8 custom-call.29
  452.9 11.7 %cholesky.343 = f32[128,128]{1,0:T(8,128)S(1)} custom-call(f32[128,128]{1,0:T(8,128)S(1)} %convolution_subtract_fusion.9), custom_call_target="Cholesky" | custom-call | tf_op jit(solution)/shard_map/jit(cholesky)/cholesky | solution.py:24
  468.7 7.7 while.4
  476.4 39.3 %custom-call.30 = f32[4,128,128]{1,2,0:T(8,128)S(1)} custom-call(f32[4,128,128]{2,1,0:T(8,128)S(1)} %get-tuple-element.18), custom_call_target="InvertDiagBlocksLowerTriangular" | custom-call | tf_op jit(solution)/shard_map/triangular_solve/custom-call.3 | solution.py:25
  531.9 7.2 fusion.19
  544.4 26.8 %all-reduce.20 = bf16[512,512]{0,1:T(8,128)(2,1)} all-reduce(f32[512,512]{0,1:T(8,128)S(1)} %convolution_bitcast_fusion.3), channel_id=1, replica_groups=mesh['tm'=8,'chan'=4] {'chan'}, use_global_device_ids=true, to_apply=%region_11.14 | all-reduce | flops 262144 | bytes 1572864 | tf_op jit(solution)/shard_map/psum | solution.py:29
  581.9 7.9 convolution_bitcast_fusion
  589.9 269.8 %all-reduce.15.cloned.1.call-done = f32[4096,512]{0,1:T(8,128)} async-done(((f32[4096,512]{0,1:T(8,128)}), f32[4096,512]{0,1:T(8,128)}) %all-reduce.15.cloned.1.call-update) | async-done | bytes 8388624 | tf_op jit(solution)/shard_map/psum | solution.py:19
  859.7 17.2 %fusion.88 = f32[512,512]{0,1:T(8,128)} fusion(f32[4096,512]{0,1:T(8,128)} %all-reduce.15.cloned.1.call-done), kind=kOutput, calls=%fused_computation.155 | convolution fusion | flops 12884901888 | bytes 9437184 | tf_op jit(solution)/shard_map/dot_general | solution.py:20
  877.1 36.6 %all-reduce.17.cloned.1.call-done = f32[512,512]{0,1:T(8,128)} async-done(((f32[512,512]{0,1:T(8,128)}), f32[512,512]{0,1:T(8,128)}) %all-reduce.17.cloned.1.call-update) | async-done | bytes 1048592 | tf_op jit(solution)/shard_map/psum | solution.py:23
  916.7 11.7 %cholesky.358 = f32[128,128]{1,0:T(8,128)S(1)} custom-call(f32[128,128]{1,0:T(8,128)S(1)} %cholesky.439), custom_call_target="Cholesky" | custom-call | tf_op jit(solution)/shard_map/jit(cholesky)/cholesky | solution.py:24
  928.6 9.8 custom-call.31
  939.1 11.7 %cholesky.377 = f32[128,128]{1,0:T(8,128)S(1)} custom-call(f32[128,128]{1,0:T(8,128)S(1)} %cholesky.443), custom_call_target="Cholesky" | custom-call | tf_op jit(solution)/shard_map/jit(cholesky)/cholesky | solution.py:24
  952.1 10.2 custom-call.32
  963.0 11.7 %cholesky.398 = f32[128,128]{1,0:T(8,128)S(1)} custom-call(f32[128,128]{1,0:T(8,128)S(1)} %cholesky.448), custom_call_target="Cholesky" | custom-call | tf_op jit(solution)/shard_map/jit(cholesky)/cholesky | solution.py:24
  975.4 9.8 custom-call.33
  985.8 11.7 %cholesky.415 = f32[128,128]{1,0:T(8,128)S(1)} custom-call(f32[128,128]{1,0:T(8,128)S(1)} %convolution_subtract_fusion.8), custom_call_target="Cholesky" | custom-call | tf_op jit(solution)/shard_map/jit(cholesky)/cholesky | solution.py:24
  1000.9 7.7 while.5
  1008.6 39.3 %custom-call.34 = f32[4,128,128]{1,2,0:T(8,128)S(1)} custom-call(f32[4,128,128]{2,1,0:T(8,128)S(1)} %get-tuple-element.19), custom_call_target="InvertDiagBlocksLowerTriangular" | custom-call | tf_op jit(solution)/shard_map/triangular_solve/custom-call.3 | solution.py:25
  1064.0 7.0 fusion.16
  1076.4 36.6 %all-reduce.19.cloned.1.call-done = f32[512,512]{0,1:T(8,128)} async-done(((f32[512,512]{0,1:T(8,128)}), f32[512,512]{0,1:T(8,128)}) %all-reduce.19.cloned.1.call-update) | async-done | bytes 1048592 | tf_op jit(solution)/shard_map/psum | solution.py:29
  (118 shorter events, 99.3 us)
Async XLA Ops:
  7.2 43.4 %all-reduce.9.cloned.1.call-start = ((), (), s32[]{:S(2)}) async-start(), calls=%async_computation | async-start | bytes 2097152 | tf_op jit(solution)/shard_map/psum | solution.py:11
  14.0 314.1 %all-reduce.11.cloned.1.call-start = ((), (), s32[]{:S(2)}) async-start(), calls=%async_computation.1 | async-start | bytes 16777216 | tf_op jit(solution)/shard_map/psum | solution.py:19
  58.7 323.5 %all-reduce.13.cloned.1.call-start = ((), (), s32[]{:S(2)}) async-start(), calls=%async_computation.2 | async-start | bytes 2097152 | tf_op jit(solution)/shard_map/psum | solution.py:23
  345.3 514.3 %all-reduce.15.cloned.1.call-start = ((), (), s32[]{:S(2)}) async-start(), calls=%async_computation.3 | async-start | bytes 16777216 | tf_op jit(solution)/shard_map/psum | solution.py:19
  524.9 16.1 %copy-start.1 = (f32[4096,128]{0,1:T(8,128)}, f32[4096,128]{0,1:T(8,128)S(1)}, u32[]{:S(2)}) copy-start(f32[4096,128]{0,1:T(8,128)S(1)} %fusion.62) | copy-start | bytes 6291460
  531.8 9.2 copy-start.5
  531.9 10.2 copy-start.2
  541.0 1.0 copy-start.7
  571.2 10.8 copy-start.6
  589.8 323.9 %all-reduce.17.cloned.1.call-start = ((), (), s32[]{:S(2)}) async-start(), calls=%async_computation.4 | async-start | bytes 2097152 | tf_op jit(solution)/shard_map/psum | solution.py:23
  876.9 236.2 %all-reduce.19.cloned.1.call-start = ((), (), s32[]{:S(2)}) async-start(), calls=%async_computation.5 | async-start | bytes 2097152 | tf_op jit(solution)/shard_map/psum | solution.py:29
  1057.1 15.9 %copy-start = (f32[4096,128]{0,1:T(8,128)}, f32[4096,128]{0,1:T(8,128)S(1)}, u32[]{:S(2)}) copy-start(f32[4096,128]{0,1:T(8,128)S(1)} %fusion.56) | copy-start | bytes 6291460
  1064.0 9.0 copy-start.4
  1064.0 9.0 copy-start.3
Sparse Core Ops, SparseCore 0:
  14.1 36.3 all-reduce.8
  58.8 269.2 all-reduce.10
  345.5 36.6 all-reduce.12
  589.9 269.6 all-reduce.14
  877.0 36.6 all-reduce.16
  1076.6 36.4 all-reduce.18
where the time goes:
time: 1140 us; the launch traced here: 1130 us
  waiting for transfers between devices  686 us (60%)
  other arithmetic  241 us (21%)
  matrix products  128 us (11%)
  blocking collectives  37.8 us (3%)
  local copies, waits for them, and re-layouts  22.2 us (2%)
  between operations  19.7 us (2%)
    psum x2, waiting for transfers between devices, shards(): factor = lax.psum(local_factor, 'tm')  539 us
    another operation x29, other arithmetic, shards(): lower = jnp.linalg.cholesky(gram)  158 us
    another operation x5, other arithmetic, shards(): lax.linalg.triangular_solve(lower, factor, left_side=False, lower=True, t...  79.2 us
    psum x2, waiting for transfers between devices, shards(): gram = lax.psum(local_gram, 'chan')  73.1 us
    another operation x14, matrix products, shards(): lax.linalg.triangular_solve(lower, factor, left_side=False, lower=True, t...  50.1 us
    psum x1, waiting for transfers between devices, shards(): coords = lax.psum(local_coords, 'chan')  36.6 us
    psum x1, waiting for transfers between devices, shards(): lax.psum(jnp.dot(samples, sketch, preferred_element_type=jnp.float32), 'c...  36.5 us
    dot_general x2, matrix products, shards(): jnp.dot(factor.T, factor, precision=lax.Precision.HIGHEST, preferred_elem...  34.5 us
  transfers between devices with their start and end apart: 6, of which 6 were waited for; matrix products, arithmetic and copies ran while one was open for 0% of the time, Pallas kernels for 0%

commit v1 on v0

v1 whole, which is shorter than its diff:
```python
import jax
import jax.numpy as jnp
from jax import lax
from jax.sharding import PartitionSpec as P

ROUNDS = 2


def shards(samples, sketch, channels):
    rows, rank = samples.shape[0], sketch.shape[1]
    f32 = jnp.float32
    wide = samples.astype(f32)
    norms = jnp.sum(wide * wide, axis=1)
    local = jnp.dot(samples, sketch, preferred_element_type=f32)
    both = jnp.concatenate([local, jnp.broadcast_to(norms[:, None], (rows, 128))], axis=1)
    both = lax.psum(both, "chan")
    sketched, norms = both[:, :rank], both[:, rank]
    weights = jnp.ones((rows,), f32)
    for step in range(ROUNDS):
        weighted = ((weights * weights)[:, None] * sketched).astype(jnp.bfloat16)
        local_factor = jnp.einsum("sc,sk->ck", samples, weighted, preferred_element_type=f32)
        part = lax.psum_scatter(local_factor.astype(jnp.bfloat16), "tm", scatter_dimension=0, tiled=True)
        factor = lax.all_gather(part, "tm", axis=0, tiled=True)
        gram = jnp.einsum("ck,cl->kl", factor, factor, preferred_element_type=f32)
        seen = jnp.dot(samples, factor, preferred_element_type=f32)
        both = lax.psum(jnp.concatenate([gram, seen], axis=0), "chan")
        gram, seen = both[:rank], both[rank:]
        lower = jnp.linalg.cholesky(gram)
        coords = lax.linalg.triangular_solve(lower, seen, left_side=False, lower=True, transpose_a=True)
        energy = jnp.maximum(norms - jnp.sum(coords * coords, axis=1), 0.0)
        weights = jnp.minimum(1.0, 3.0 / jnp.sqrt(energy / channels + 1e-06))
    return (coords, weights)


def solution(mesh):
    in_specs = (P("tm", "chan"), P("chan", None))
    out_specs = (P("tm", None), P("tm"))

    def whole(samples, sketch):
        f = lambda a, b: shards(a, b, samples.shape[1])
        return jax.shard_map(f, mesh=mesh, in_specs=in_specs, out_specs=out_specs, check_vma=False)(samples, sketch)

    return whole
```

time: 1140 us -> 839 us (0.74)
  waiting for transfers between devices: 686 us -> 469 us
  matrix products: 128 us -> 55.3 us
  blocking collectives: 37.8 us -> 0 us
  local copies, waits for them, and re-layouts: 22.2 us -> 35 us
    psum x6 -> x3, waiting for transfers between devices: 685 us -> 140 us  [the longest x2 101 us: shards(): both = lax.psum(jnp.concatenate([gram, seen], axis=0), 'chan')]
    reduce_scatter x0 -> x2, waiting for transfers between devices: none -> 177 us  [shards(): lax.psum_scatter(local_factor.astype(jnp.bfloat16), 'tm', scatter_dimensi...]
    all_gather x0 -> x2, waiting for transfers between devices: none -> 152 us  [shards(): factor = lax.all_gather(part, 'tm', axis=0, tiled=True)]
    dot_general x9 -> x7, matrix products: 74 us -> 32.3 us  [the longest x2 11.9 us: shards(): seen = jnp.dot(samples, factor, preferred_element_type=f32)]
    another operation x14, matrix products: 50.1 us -> 11.8 us  [shards(): lax.linalg.triangular_solve(lower, seen, left_side=False, lower=True, tra...]
    psum x3 -> x0, blocking collectives: 37.8 us -> none  [the longest x1 26.8 us: shards(): coords = lax.psum(local_coords, 'chan')]
  transfers between devices with their start and end apart: 6 -> 7, of which waited for: 6 -> 7; matrix products, arithmetic and copies ran while one was open for 0% -> 0% of each run, Pallas kernels for 0% -> 0%
where the time goes in v1:
time: 839 us; the launch traced here: 829 us
  waiting for transfers between devices  469 us (56%)
  other arithmetic  248 us (30%)
  matrix products  55.3 us (7%)
  local copies, waits for them, and re-layouts  35 us (4%)
  between operations  20.2 us (2%)
    reduce_scatter x2, waiting for transfers between devices, shards(): lax.psum_scatter(local_factor.astype(jnp.bfloat16), 'tm', scatter_dimensi...  177 us
    another operation x29, other arithmetic, shards(): lower = jnp.linalg.cholesky(gram)  158 us
    all_gather x2, waiting for transfers between devices, shards(): factor = lax.all_gather(part, 'tm', axis=0, tiled=True)  152 us
    psum x2, waiting for transfers between devices, shards(): both = lax.psum(jnp.concatenate([gram, seen], axis=0), 'chan')  101 us
    another operation x5, other arithmetic, shards(): lax.linalg.triangular_solve(lower, seen, left_side=False, lower=True, tra...  80.8 us
    psum x1, waiting for transfers between devices, shards(): both = lax.psum(both, 'chan')  39.2 us
    another operation x27, local copies, waits for them, and re-layouts, shards(): lax.linalg.triangular_solve(lower, seen, left_side=False, lower=True, tra...  23.3 us
  transfers between devices with their start and end apart: 7, of which 7 were waited for; matrix products, arithmetic and copies ran while one was open for 0% of the time, Pallas kernels for 0%

profile of v1, /device:TPU:29, one launch (start us, length us, event | category | flops | bytes accessed | tf_op | source)
XLA Modules:
  0.0 828.5 jit_solution(8468604616008280250)
XLA Ops:
  7.2 3.2 multiply_reduce_fusion
  10.7 4.6 fusion.75
  16.5 39.2 %all-reduce.5.cloned.1.call-done = f32[512,640]{0,1:T(8,128)} async-done(((f32[512,640]{0,1:T(8,128)}), f32[512,640]{0,1:T(8,128)}) %all-reduce.5.cloned.1.call-update) | async-done | bytes 1310736 | tf_op jit(solution)/shard_map/psum | solution.py:16
  55.8 6.8 fusion
  62.6 88.4 %reduce-scatter.3.cloned.1.call-done = bf16[512,512]{0,1:T(8,128)(2,1)} async-done(((bf16[4096,512]{0,1:T(8,128)(2,1)}), bf16[512,512]{0,1:T(8,128)(2,1)}) %reduce-scatter.3.cloned.1.call-update) | async-done | bytes 524304 | tf_op jit(solution)/shard_map/reduce_scatter | solution.py:22
  151.1 76.2 %all-gather.3.cloned.1.call-done = bf16[4096,512]{0,1:T(8,128)(2,1)} async-done(((bf16[512,512]{0,1:T(8,128)(2,1)}), bf16[4096,512]{0,1:T(8,128)(2,1)}) %all-gather.3.cloned.1.call-update) | async-done | bytes 4194320 | tf_op jit(solution)/shard_map/all_gather | solution.py:23
  227.4 6.0 convolution_bitcast_fusion.1
  237.4 50.4 %all-reduce.7.cloned.1.call-done = f32[1024,512]{0,1:T(8,128)} async-done(((f32[1024,512]{0,1:T(8,128)}), f32[1024,512]{0,1:T(8,128)}) %all-reduce.7.cloned.1.call-update) | async-done | bytes 2097168 | tf_op jit(solution)/shard_map/psum | solution.py:26
  287.8 2.4 slice.171
  293.0 11.7 %cholesky.286 = f32[128,128]{1,0:T(8,128)S(1)} custom-call(f32[128,128]{1,0:T(8,128)S(1)} %cholesky.426), custom_call_target="Cholesky" | custom-call | tf_op jit(solution)/shard_map/jit(cholesky)/cholesky | solution.py:28
  304.8 9.8 %custom-call.27 = f32[1,128,128]{1,2,0:T(8,128)S(1)} custom-call(f32[1,128,128]{2,1,0:T(8,128)S(1)} %get-tuple-element.65), custom_call_target="InvertDiagBlocksLowerTriangular" | custom-call | tf_op jit(solution)/shard_map/jit(cholesky)/cholesky | solution.py:28
  317.3 11.7 %cholesky.305 = f32[128,128]{1,0:T(8,128)S(1)} custom-call(f32[128,128]{1,0:T(8,128)S(1)} %cholesky.430), custom_call_target="Cholesky" | custom-call | tf_op jit(solution)/shard_map/jit(cholesky)/cholesky | solution.py:28
  329.0 10.0 %custom-call.28 = f32[1,128,128]{1,2,0:T(8,128)S(1)} custom-call(f32[1,128,128]{2,1,0:T(8,128)S(1)} %get-tuple-element.62), custom_call_target="InvertDiagBlocksLowerTriangular" | custom-call | tf_op jit(solution)/shard_map/jit(cholesky)/cholesky | solution.py:28
  340.6 11.7 %cholesky.326 = f32[128,128]{1,0:T(8,128)S(1)} custom-call(f32[128,128]{1,0:T(8,128)S(1)} %cholesky.435), custom_call_target="Cholesky" | custom-call | tf_op jit(solution)/shard_map/jit(cholesky)/cholesky | solution.py:28
  353.1 9.8 %custom-call.29 = f32[1,128,128]{1,2,0:T(8,128)S(1)} custom-call(f32[1,128,128]{2,1,0:T(8,128)S(1)} %get-tuple-element.59), custom_call_target="InvertDiagBlocksLowerTriangular" | custom-call | tf_op jit(solution)/shard_map/jit(cholesky)/cholesky | solution.py:28
  364.3 11.7 %cholesky.343 = f32[128,128]{1,0:T(8,128)S(1)} custom-call(f32[128,128]{1,0:T(8,128)S(1)} %convolution_subtract_fusion.11), custom_call_target="Cholesky" | custom-call | tf_op jit(solution)/shard_map/jit(cholesky)/cholesky | solution.py:28
  381.4 11.7 %while.4 = (s32[]{:T(128)}, f32[512,512]{1,0:T(8,128)}, s32[4,2]{0,1:T(2,128)S(1)}, f32[4,128,128]{2,1,0:T(8,128)S(1)}, s32[]{:T(128)}) while((s32[]{:T(128)}, f32[512,512]{1,0:T(8,128)}, s32[4,2]{0,1:T(2,128)S(1)}, f32[4,128,128]{2,1,0:T(8,128)S(1)}, s32[]{:T(128)}) %tuple.58), condition=%wide.while_cond, body=%wide.while_body.sunk | while | flops 2 | bytes 131181 | solution.py:29
  393.1 39.3 %custom-call.30 = f32[4,128,128]{1,2,0:T(8,128)S(1)} custom-call(f32[4,128,128]{2,1,0:T(8,128)S(1)} %get-tuple-element.18), custom_call_target="InvertDiagBlocksLowerTriangular" | custom-call | tf_op jit(solution)/shard_map/triangular_solve/custom-call.3 | solution.py:29
  438.7 4.3 fusion.1
  443.1 88.5 %reduce-scatter.5.cloned.1.call-done = bf16[512,512]{0,1:T(8,128)(2,1)} async-done(((bf16[4096,512]{0,1:T(8,128)(2,1)}), bf16[512,512]{0,1:T(8,128)(2,1)}) %reduce-scatter.5.cloned.1.call-update) | async-done | bytes 524304 | tf_op jit(solution)/shard_map/reduce_scatter | solution.py:22
  531.8 75.9 %all-gather.5.cloned.1.call-done = bf16[4096,512]{0,1:T(8,128)(2,1)} async-done(((bf16[512,512]{0,1:T(8,128)(2,1)}), bf16[4096,512]{0,1:T(8,128)(2,1)}) %all-gather.5.cloned.1.call-update) | async-done | bytes 4194320 | tf_op jit(solution)/shard_map/all_gather | solution.py:23
  607.7 6.0 convolution_bitcast_fusion
  617.5 50.7 %all-reduce.9.cloned.1.call-done = f32[1024,512]{0,1:T(8,128)} async-done(((f32[1024,512]{0,1:T(8,128)}), f32[1024,512]{0,1:T(8,128)}) %all-reduce.9.cloned.1.call-update) | async-done | bytes 2097168 | tf_op jit(solution)/shard_map/psum | solution.py:26
  673.4 11.7 %cholesky.358 = f32[128,128]{1,0:T(8,128)S(1)} custom-call(f32[128,128]{1,0:T(8,128)S(1)} %cholesky.439), custom_call_target="Cholesky" | custom-call | tf_op jit(solution)/shard_map/jit(cholesky)/cholesky | solution.py:28
  685.3 9.8 %custom-call.31 = f32[1,128,128]{1,2,0:T(8,128)S(1)} custom-call(f32[1,128,128]{2,1,0:T(8,128)S(1)} %get-tuple-element.55), custom_call_target="InvertDiagBlocksLowerTriangular" | custom-call | tf_op jit(solution)/shard_map/jit(cholesky)/cholesky | solution.py:28
  697.6 11.9 %cholesky.377 = f32[128,128]{1,0:T(8,128)S(1)} custom-call(f32[128,128]{1,0:T(8,128)S(1)} %cholesky.443), custom_call_target="Cholesky" | custom-call | tf_op jit(solution)/shard_map/jit(cholesky)/cholesky | solution.py:28
  710.9 9.8 %custom-call.32 = f32[1,128,128]{1,2,0:T(8,128)S(1)} custom-call(f32[1,128,128]{2,1,0:T(8,128)S(1)} %get-tuple-element.52), custom_call_target="InvertDiagBlocksLowerTriangular" | custom-call | tf_op jit(solution)/shard_map/jit(cholesky)/cholesky | solution.py:28
  722.3 11.7 %cholesky.398 = f32[128,128]{1,0:T(8,128)S(1)} custom-call(f32[128,128]{1,0:T(8,128)S(1)} %cholesky.448), custom_call_target="Cholesky" | custom-call | tf_op jit(solution)/shard_map/jit(cholesky)/cholesky | solution.py:28
  734.7 9.8 %custom-call.33 = f32[1,128,128]{1,2,0:T(8,128)S(1)} custom-call(f32[1,128,128]{2,1,0:T(8,128)S(1)} %get-tuple-element.49), custom_call_target="InvertDiagBlocksLowerTriangular" | custom-call | tf_op jit(solution)/shard_map/jit(cholesky)/cholesky | solution.py:28
  746.2 11.7 %cholesky.415 = f32[128,128]{1,0:T(8,128)S(1)} custom-call(f32[128,128]{1,0:T(8,128)S(1)} %convolution_subtract_fusion.10), custom_call_target="Cholesky" | custom-call | tf_op jit(solution)/shard_map/jit(cholesky)/cholesky | solution.py:28
  762.3 11.7 %while.5 = (s32[]{:T(128)}, f32[512,512]{1,0:T(8,128)}, s32[4,2]{0,1:T(2,128)S(1)}, f32[4,128,128]{2,1,0:T(8,128)S(1)}, s32[]{:T(128)}) while((s32[]{:T(128)}, f32[512,512]{1,0:T(8,128)}, s32[4,2]{0,1:T(2,128)S(1)}, f32[4,128,128]{2,1,0:T(8,128)S(1)}, s32[]{:T(128)}) %tuple.78), condition=%wide.while_cond.clone, body=%wide.while_body.clone.sunk | while | flops 2 | bytes 131181 | solution.py:29
  774.0 39.3 %custom-call.34 = f32[4,128,128]{1,2,0:T(8,128)S(1)} custom-call(f32[4,128,128]{2,1,0:T(8,128)S(1)} %get-tuple-element.19), custom_call_target="InvertDiagBlocksLowerTriangular" | custom-call | tf_op jit(solution)/shard_map/triangular_solve/custom-call.3 | solution.py:29
  (127 shorter events, 74.1 us)
Async XLA Ops:
  7.2 48.6 %all-reduce.5.cloned.1.call-start = ((), (), s32[]{:S(2)}) async-start(), calls=%async_computation.2 | async-start | bytes 2621440 | tf_op jit(solution)/shard_map/psum | solution.py:16
  7.2 3.5 copy-start.2
  16.5 134.6 %reduce-scatter.3.cloned.1.call-start = ((), (), s32[]{:S(2)}) async-start(), calls=%async_computation.3 | async-start | bytes 4718592 | tf_op jit(solution)/shard_map/reduce_scatter | solution.py:22
  62.6 164.8 %all-gather.3.cloned.1.call-start = ((), (), s32[]{:S(2)}) async-start(), calls=%async_computation.4 | async-start | bytes 4718592 | tf_op jit(solution)/shard_map/all_gather | solution.py:23
  151.1 136.8 %all-reduce.7.cloned.1.call-start = ((), (), s32[]{:S(2)}) async-start(), calls=%async_computation.5 | async-start | bytes 4194304 | tf_op jit(solution)/shard_map/psum | solution.py:26
  227.4 6.0 copy-start.7
  237.2 294.4 %reduce-scatter.5.cloned.1.call-start = ((), (), s32[]{:S(2)}) async-start(), calls=%async_computation.6 | async-start | bytes 4718592 | tf_op jit(solution)/shard_map/reduce_scatter | solution.py:22
  287.8 4.0 copy-start
  292.1 1.0 copy-start.5
  432.4 6.2 copy-start.6
  432.5 6.2 copy-start.3
  443.0 164.7 %all-gather.5.cloned.1.call-start = ((), (), s32[]{:S(2)}) async-start(), calls=%async_computation.7 | async-start | bytes 4718592 | tf_op jit(solution)/shard_map/all_gather | solution.py:23
  531.6 136.6 %all-reduce.9.cloned.1.call-start = ((), (), s32[]{:S(2)}) async-start(), calls=%async_computation.8 | async-start | bytes 4194304 | tf_op jit(solution)/shard_map/psum | solution.py:26
  607.7 6.0 copy-start.8
  668.2 4.0 copy-start.1
  672.4 1.0 copy-start.4
Sparse Core Ops, SparseCore 0:
  16.6 39.1 all-reduce.4
  62.7 88.3 reduce-scatter.2
  153.3 73.9 all-gather.2
  237.3 50.5 all-reduce.6
  443.1 88.3 reduce-scatter.4
  533.7 73.9 all-gather.4
  617.6 50.5 all-reduce.8

commit v2 on v1

v2 whole, which is shorter than its diff:
```python
import functools

import jax
import jax.numpy as jnp
from jax import lax
from jax.experimental import pallas as pl
from jax.experimental.pallas import tpu as pltpu
from jax.sharding import PartitionSpec as P

ROUNDS = 2
B = 128
HIGH = lax.Precision.HIGHEST


def dot_t(a, b):
    return lax.dot_general(a, b, (((1,), (1,)), ((), ())), precision=HIGH, preferred_element_type=jnp.float32)


def invert_block(block, inv_ref):
    eye = lax.broadcasted_iota(jnp.int32, (B, B), 0) == lax.broadcasted_iota(jnp.int32, (B, B), 1)
    left, right = block, eye.astype(jnp.float32)
    top = 0
    for j in range(B):
        cut = (j // 8) * 8 - top
        if cut:
            left, right, top = left[cut:], right[cut:], top + cut
        k = j - top
        scale = lax.rsqrt(left[k : k + 1, j : j + 1])
        row_left = left[k : k + 1, :] * scale
        row_right = right[k : k + 1, :] * scale
        inv_ref[j : j + 1, :] = row_right
        if j + 1 < B:
            col = left[:, j : j + 1] * scale
            left = left - col * row_left
            right = right - col * row_right


def fit_kernel(channels, both_ref, sketched_ref, norms_ref, coords_ref, weights_ref, weighted_ref, work, inv):
    rank = coords_ref.shape[1]
    total = work.shape[0]
    work[...] = both_ref[...]

    def block_step(b, carry):
        at = pl.multiple_of(b * B, B)
        invert_block(work[pl.ds(at, B), pl.ds(at, B)], inv)
        for k in range(rank // B):

            @pl.when(b == k)
            def _():
                lo, hi = k * B, (k + 1) * B
                panel = dot_t(work[hi:, lo:hi], inv[...])
                coords_ref[:, lo:hi] = panel[rank - hi :]
                if hi < rank:
                    work[hi:, hi:] = work[hi:, hi:] - dot_t(panel, panel[: rank - hi])

        return carry

    lax.fori_loop(0, rank // B, block_step, 0)
    coords = coords_ref[...]
    energy = jnp.maximum(norms_ref[:, :1] - jnp.sum(coords * coords, axis=1, keepdims=True), 0.0)
    weights = jnp.minimum(1.0, 3.0 / jnp.sqrt(energy / channels + 1e-06))
    weights_ref[...] = weights
    weighted_ref[...] = ((weights * weights) * sketched_ref[...]).astype(jnp.bfloat16)


def fit(channels, both, sketched, norms):
    rows, rank = sketched.shape
    return pl.pallas_call(
        functools.partial(fit_kernel, channels),
        out_shape=(
            jax.ShapeDtypeStruct((rows, rank), jnp.float32),
            jax.ShapeDtypeStruct((rows, 1), jnp.float32),
            jax.ShapeDtypeStruct((rows, rank), jnp.bfloat16),
        ),
        scratch_shapes=[pltpu.VMEM(both.shape, jnp.float32), pltpu.VMEM((B, B), jnp.float32)],
        compiler_params=pltpu.CompilerParams(vmem_limit_bytes=32 * 1024 * 1024),
    )(both, sketched, norms)


def shards(samples, sketch, channels):
    rows, rank = samples.shape[0], sketch.shape[1]
    f32 = jnp.float32
    wide = samples.astype(f32)
    norms = jnp.sum(wide * wide, axis=1)
    local = jnp.dot(samples, sketch, preferred_element_type=f32)
    both = jnp.concatenate([local, jnp.broadcast_to(norms[:, None], (rows, 128))], axis=1)
    both = lax.psum(both, "chan")
    sketched, norms = both[:, :rank], both[:, rank:]
    weighted = sketched.astype(jnp.bfloat16)
    for step in range(ROUNDS):
        local_factor = jnp.einsum("sc,sk->ck", samples, weighted, preferred_element_type=f32)
        part = lax.psum_scatter(local_factor.astype(jnp.bfloat16), "tm", scatter_dimension=0, tiled=True)
        factor = lax.all_gather(part, "tm", axis=0, tiled=True)
        gram = jnp.einsum("ck,cl->kl", factor, factor, preferred_element_type=f32)
        seen = jnp.dot(samples, factor, preferred_element_type=f32)
        both = lax.psum(jnp.concatenate([gram, seen], axis=0), "chan")
        coords, weights, weighted = fit(channels, both, sketched, norms)
    return (coords, weights[:, 0])


def solution(mesh):
    in_specs = (P("tm", "chan"), P("chan", None))
    out_specs = (P("tm", None), P("tm"))

    def whole(samples, sketch):
        f = lambda a, b: shards(a, b, samples.shape[1])
        return jax.shard_map(f, mesh=mesh, in_specs=in_specs, out_specs=out_specs, check_vma=False)(samples, sketch)

    return whole
```

time: 839 us -> 632 us (0.75)
  other arithmetic: 248 us -> 8.08 us
  Pallas kernels: 0 us -> 98.6 us
  local copies, waits for them, and re-layouts: 35 us -> 3.74 us
  matrix products: 55.3 us -> 34.5 us
    another operation x34 -> x0, other arithmetic: 239 us -> none  [the longest x29 158 us: shards(): lower = jnp.linalg.cholesky(gram)]
    pallas_call x0 -> x2, Pallas kernels: none -> 98.6 us  [fit(): pl.pallas_call(functools.partial(fit_kernel, channels), out_shape=(jax.Sh...]
    another operation x35 -> x0, local copies, waits for them, and re-layouts: 23.6 us -> none  [the longest x27 23.3 us: shards(): lax.linalg.triangular_solve(lower, seen, left_side=False, lower=True, tra...]
    another operation x26 -> x0, matrix products: 23 us -> none  [the longest x14 11.8 us: shards(): lax.linalg.triangular_solve(lower, seen, left_side=False, lower=True, tra...]
where the time goes in v2:
time: 632 us; the launch traced here: 629 us
  waiting for transfers between devices  469 us (74%)
  Pallas kernels  98.6 us (16%)
  matrix products  34.5 us (5%)
  between operations  14.2 us (2%)
  other arithmetic  8.08 us (1%)
    reduce_scatter x2, waiting for transfers between devices, shards(): lax.psum_scatter(local_factor.astype(jnp.bfloat16), 'tm', scatter_dimensi...  177 us
    all_gather x2, waiting for transfers between devices, shards(): factor = lax.all_gather(part, 'tm', axis=0, tiled=True)  152 us
    psum x2, waiting for transfers between devices, shards(): both = lax.psum(jnp.concatenate([gram, seen], axis=0), 'chan')  101 us
    pallas_call x2, Pallas kernels, fit(): pl.pallas_call(functools.partial(fit_kernel, channels), out_shape=(jax.Sh...  98.6 us
    psum x1, waiting for transfers between devices, shards(): both = lax.psum(both, 'chan')  39.2 us
    dot_general x2, matrix products, shards(): jnp.einsum('sc,sk->ck', samples, weighted, preferred_element_type=f32)  13.3 us
  transfers between devices with their start and end apart: 7, of which 7 were waited for; matrix products, arithmetic and copies ran while one was open for 0% of the time, Pallas kernels for 0%

profile of v2, /device:TPU:29, one launch (start us, length us, event | category | flops | bytes accessed | tf_op | source)
XLA Modules:
  0.0 628.8 jit_solution(11789741679220804622)
XLA Ops:
  7.2 3.2 multiply_reduce_fusion
  10.5 0.2 copy-done.2
  10.7 4.5 fusion.4
  15.2 0.1 broadcast_in_dim.2
  15.3 1.2 pad_maximum_fusion.2
  16.5 0.0 reduce-scatter.3.cloned.1.call-start
  16.6 39.2 %all-reduce.4.cloned.1.call-done = f32[512,640]{1,0:T(8,128)} async-done(((f32[512,640]{1,0:T(8,128)}), f32[512,640]{1,0:T(8,128)}) %all-reduce.4.cloned.1.call-update) | async-done | bytes 1310736 | tf_op jit(solution)/shard_map/psum | solution.py:87
  55.8 6.8 %fusion = bf16[4096,512]{0,1:T(8,128)(2,1)} fusion(bf16[512,4096]{1,0:T(8,128)(2,1)} %param.2, f32[512,640]{1,0:T(8,128)} %all-reduce.4.cloned.1.call-done), kind=kOutput, calls=%fused_computation.3 | convolution fusion | flops 2149580800 | bytes 8912896 | tf_op jit(solution)/shard_map/sc,sk->ck/dot_general | solution.py:91
  62.7 0.0 all-gather.3.cloned.1.call-start
  62.7 88.2 %reduce-scatter.3.cloned.1.call-done = bf16[512,512]{0,1:T(8,128)(2,1)} async-done(((bf16[4096,512]{0,1:T(8,128)(2,1)}), bf16[512,512]{0,1:T(8,128)(2,1)}) %reduce-scatter.3.cloned.1.call-update) | async-done | bytes 524304 | tf_op jit(solution)/shard_map/reduce_scatter | solution.py:92
  151.0 76.2 %all-gather.3.cloned.1.call-done = bf16[4096,512]{0,1:T(8,128)(2,1)} async-done(((bf16[512,512]{0,1:T(8,128)(2,1)}), bf16[4096,512]{0,1:T(8,128)(2,1)}) %all-gather.3.cloned.1.call-update) | async-done | bytes 4194320 | tf_op jit(solution)/shard_map/all_gather | solution.py:93
  227.3 6.0 convolution_bitcast_fusion.1
  233.2 2.4 fusion.5
  235.6 1.5 pad_maximum_fusion
  237.1 0.2 reduce-scatter.5.cloned.1.call-start
  237.3 0.1 copy-done.3
  237.4 0.1 slice.8.sketched_ref
  237.6 50.2 %all-reduce.6.cloned.1.call-done.both_ref = f32[1024,512]{1,0:T(8,128)} async-done(((f32[1024,512]{1,0:T(8,128)}), f32[1024,512]{1,0:T(8,128)}) %all-reduce.6.cloned.1.call-update) | async-done | bytes 2097168 | tf_op jit(solution)/shard_map/psum | solution.py:96
  287.8 1.6 copy-done
  289.4 49.2 %shard_map.41 = (f32[512,512]{1,0:T(8,128)}, f32[512,1]{1,0:T(8,128)}, bf16[512,512]{1,0:T(8,128)(2,1)S(1)}) custom-call(f32[1024,512]{1,0:T(8,128)S(1)} %copy-done, f32[512,512]{1,0:T(8,128)S(1)} %slice.8.sketched_ref, f32[512,128]{1,0:T(8,128)S(1)} %slice.9.norms_ref), custom_call_target="tpu_custom_call" | custom-call | tf_op jit(solution)/shard_map/pallas_call | solution.py:68
  338.6 6.5 %fusion.1 = bf16[4096,512]{0,1:T(8,128)(2,1)} fusion(bf16[512,512]{1,0:T(8,128)(2,1)S(1)} %get-tuple-element.5, bf16[512,4096]{1,0:T(8,128)(2,1)} %param.2), kind=kOutput, calls=%fused_computation.4 | convolution fusion | flops 2149580800 | bytes 8912896 | tf_op jit(solution)/shard_map/sc,sk->ck/dot_general | solution.py:91
  345.1 0.0 all-gather.5.cloned.1.call-start
  345.2 88.5 %reduce-scatter.5.cloned.1.call-done = bf16[512,512]{0,1:T(8,128)(2,1)} async-done(((bf16[4096,512]{0,1:T(8,128)(2,1)}), bf16[512,512]{0,1:T(8,128)(2,1)}) %reduce-scatter.5.cloned.1.call-update) | async-done | bytes 524304 | tf_op jit(solution)/shard_map/reduce_scatter | solution.py:92
  433.6 0.3 all-reduce.8.cloned.1.call-start
  433.9 75.8 %all-gather.5.cloned.1.call-done = bf16[4096,512]{0,1:T(8,128)(2,1)} async-done(((bf16[512,512]{0,1:T(8,128)(2,1)}), bf16[4096,512]{0,1:T(8,128)(2,1)}) %all-gather.5.cloned.1.call-update) | async-done | bytes 4194320 | tf_op jit(solution)/shard_map/all_gather | solution.py:93
  509.8 6.0 convolution_bitcast_fusion
  515.7 2.4 fusion.6
  518.1 1.5 pad_maximum_fusion.1
  519.6 50.7 %all-reduce.8.cloned.1.call-done.both_ref = f32[1024,512]{1,0:T(8,128)} async-done(((f32[1024,512]{1,0:T(8,128)}), f32[1024,512]{1,0:T(8,128)}) %all-reduce.8.cloned.1.call-update) | async-done | bytes 2097168 | tf_op jit(solution)/shard_map/psum | solution.py:96
  570.3 1.6 copy-done.1
  571.9 49.3 %shard_map.42 = (f32[512,512]{1,0:T(8,128)}, f32[512,1]{1,0:T(8,128)S(1)}, bf16[512,512]{1,0:T(8,128)(2,1)}) custom-call(f32[1024,512]{1,0:T(8,128)S(1)} %copy-done.1, f32[512,512]{1,0:T(8,128)S(1)} %slice.8.sketched_ref, f32[512,128]{1,0:T(8,128)S(1)} %slice.9.norms_ref), custom_call_target="tpu_custom_call" | custom-call | tf_op jit(solution)/shard_map/pallas_call | solution.py:68
  621.2 0.7 reduce
  (18 shorter events, 0.2 us)
Async XLA Ops:
  7.2 48.7 %all-reduce.4.cloned.1.call-start = ((), (), s32[]{:S(2)}) async-start(), calls=%async_computation.2 | async-start | bytes 2621440 | tf_op jit(solution)/shard_map/psum | solution.py:87
  7.2 3.5 copy-start.2
  16.5 134.4 %reduce-scatter.3.cloned.1.call-start = ((), (), s32[]{:S(2)}) async-start(), calls=%async_computation.3 | async-start | bytes 4718592 | tf_op jit(solution)/shard_map/reduce_scatter | solution.py:92
  62.7 164.6 %all-gather.3.cloned.1.call-start = ((), (), s32[]{:S(2)}) async-start(), calls=%async_computation.4 | async-start | bytes 4718592 | tf_op jit(solution)/shard_map/all_gather | solution.py:93
  151.0 136.8 %all-reduce.6.cloned.1.call-start = ((), (), s32[]{:S(2)}) async-start(), calls=%async_computation.5 | async-start | bytes 4194304 | tf_op jit(solution)/shard_map/psum | solution.py:96
  227.3 6.0 copy-start.4
  235.6 1.8 copy-start.3
  237.1 196.5 %reduce-scatter.5.cloned.1.call-start = ((), (), s32[]{:S(2)}) async-start(), calls=%async_computation.6 | async-start | bytes 4718592 | tf_op jit(solution)/shard_map/reduce_scatter | solution.py:92
  287.8 1.6 copy-start
  345.1 164.6 %all-gather.5.cloned.1.call-start = ((), (), s32[]{:S(2)}) async-start(), calls=%async_computation.7 | async-start | bytes 4718592 | tf_op jit(solution)/shard_map/all_gather | solution.py:93
  433.6 136.6 %all-reduce.8.cloned.1.call-start = ((), (), s32[]{:S(2)}) async-start(), calls=%async_computation.8 | async-start | bytes 4194304 | tf_op jit(solution)/shard_map/psum | solution.py:96
  509.8 6.0 copy-start.5
  570.3 1.6 copy-start.1
Sparse Core Ops, SparseCore 0:
  16.7 39.1 all-reduce.3
  62.8 88.1 reduce-scatter.2
  153.2 73.9 all-gather.2
  237.2 50.5 all-reduce.5
  345.2 88.3 reduce-scatter.4
  435.7 73.9 all-gather.4
  519.7 50.5 all-reduce.7

commit v3 on v2

--- a/solution.py
+++ b/solution.py
@@ -10,6 +10,7 @@
 ROUNDS = 2
 B = 128
 HIGH = lax.Precision.HIGHEST
+MESH = pl.DeviceIdType.MESH
 
 
 def dot_t(a, b):
@@ -77,7 +78,133 @@
     )(both, sketched, norms)
 
 
-def shards(samples, sketch, channels):
+def exchange_kernel(outer, inner, mine_ref, samples_ref, both_ref, whole, near, sent, far, acc, near_sem, far_sem, wide_sem, local_sem):
+    me = lax.axis_index("tm")
+    o, i = me // inner, me % inner
+    size, rank = acc.shape
+    f32 = jnp.float32
+
+    def peer_in(d):
+        return {"tm": o * inner + (i + d) % inner}
+
+    def peer_out(e):
+        return {"tm": ((o + e) % outer) * inner + i}
+
+    barrier = pltpu.get_barrier_semaphore()
+    for d in range(1, inner):
+        pl.semaphore_signal(barrier, inc=1, device_id=peer_in(d), device_id_type=MESH)
+    for e in range(1, outer):
+        pl.semaphore_signal(barrier, inc=1, device_id=peer_out(e), device_id_type=MESH)
+    pl.semaphore_wait(barrier, inner + outer - 2)
+
+    def copy(src, dst, sems, at, device):
+        return pltpu.make_async_remote_copy(
+            src_ref=src,
+            dst_ref=dst,
+            send_sem=sems.at[(0,) + at],
+            recv_sem=sems.at[(1,) + at],
+            device_id=device,
+            device_id_type=MESH,
+        )
+
+    order = list(range(1, outer)) + [0]
+    first = {}
+    for e in order:
+        row = (o + e) % outer
+        for d in range(1, inner):
+            block = row * inner + (i + d) % inner
+            first[e, d] = copy(mine_ref.at[block], near.at[e, d - 1], near_sem, (e, d - 1), peer_in(d))
+            first[e, d].start()
+    second = {}
+    for e in order:
+        for d in range(1, inner):
+            first[e, d].wait_recv()
+        total = mine_ref[((o + e) % outer) * inner + i].astype(f32)
+        for d in range(1, inner):
+            total = total + near[e, d - 1].astype(f32)
+        if e:
+            sent[e - 1] = total.astype(jnp.bfloat16)
+            second[e] = copy(sent.at[e - 1], far.at[e - 1], far_sem, (e - 1,), peer_out(e))
+            second[e].start()
+        else:
+            acc[...] = total
+    for e in range(1, outer):
+        second[e].wait_recv()
+        acc[...] = acc[...] + far[e - 1].astype(f32)
+    whole[me] = acc[...].astype(jnp.bfloat16)
+
+    def wide(e):
+        return copy(whole.at[me], whole.at[me], wide_sem, (e - 1,), peer_out(e))
+
+    def local(e, d):
+        block = ((o - e + outer) % outer) * inner + i
+        return copy(whole.at[block], whole.at[block], local_sem, (e, d - 1), peer_in(d))
+
+    for e in range(1, outer):
+        wide(e).start()
+    for d in range(1, inner):
+        local(0, d).start()
+    both_ref[...] = jnp.zeros_like(both_ref)
+
+    def use(block):
+        part = whole[block]
+        columns = pl.ds(pl.multiple_of(block * size, size), size)
+        both_ref[:rank] += lax.dot_general(part, part, (((0,), (0,)), ((), ())), preferred_element_type=f32)
+        both_ref[rank:] += jnp.dot(samples_ref[:, columns], part, preferred_element_type=f32)
+
+    use(me)
+    for e in range(1, outer):
+        block = ((o - e + outer) % outer) * inner + i
+        copy(whole.at[block], whole.at[block], wide_sem, (e - 1,), peer_out(e)).wait_recv()
+        for d in range(1, inner):
+            local(e, d).start()
+        use(block)
+    for e in range(outer):
+        for d in range(1, inner):
+            block = ((o - e + outer) % outer) * inner + (i - d + inner) % inner
+            copy(whole.at[block], whole.at[block], local_sem, (e, d - 1), peer_in(d)).wait_recv()
+            use(block)
+    for one in first.values():
+        one.wait_send()
+    for one in second.values():
+        one.wait_send()
+    for e in range(1, outer):
+        wide(e).wait_send()
+    for e in range(outer):
+        for d in range(1, inner):
+            local(e, d).wait_send()
+
+
+def exchange(mine, samples, devices):
+    rows, channels = samples.shape
+    rank = mine.shape[1]
+    outer = 4 if devices % 4 == 0 else 1
+    inner = devices // outer
+    size = channels // devices
+    low = jnp.bfloat16
+    return pl.pallas_call(
+        functools.partial(exchange_kernel, outer, inner),
+        out_shape=jax.ShapeDtypeStruct((rank + rows, rank), jnp.float32),
+        in_specs=[pl.BlockSpec(memory_space=pltpu.VMEM)] * 2,
+        out_specs=pl.BlockSpec(memory_space=pltpu.VMEM),
+        scratch_shapes=[
+            pltpu.VMEM((devices, size, rank), low),
+            pltpu.VMEM((outer, inner - 1, size, rank), low),
+            pltpu.VMEM((outer - 1, size, rank), low),
+            pltpu.VMEM((outer - 1, size, rank), low),
+            pltpu.VMEM((size, rank), jnp.float32),
+            pltpu.SemaphoreType.DMA((2, outer, inner - 1)),
+            pltpu.SemaphoreType.DMA((2, outer - 1)),
+            pltpu.SemaphoreType.DMA((2, outer - 1)),
+            pltpu.SemaphoreType.DMA((2, outer, inner - 1)),
+        ],
+        compiler_params=pltpu.CompilerParams(
+            collective_id=0, has_side_effects=True, vmem_limit_bytes=40 * 1024 * 1024
+        ),
+    )(mine.reshape(devices, size, rank), samples)
+
+
+def shards(samples, sketch, channels, devices):
     rows, rank = samples.shape[0], sketch.shape[1]
     f32 = jnp.float32
     wide = samples.astype(f32)
@@ -89,11 +216,7 @@
     weighted = sketched.astype(jnp.bfloat16)
     for step in range(ROUNDS):
         local_factor = jnp.einsum("sc,sk->ck", samples, weighted, preferred_element_type=f32)
-        part = lax.psum_scatter(local_factor.astype(jnp.bfloat16), "tm", scatter_dimension=0, tiled=True)
-        factor = lax.all_gather(part, "tm", axis=0, tiled=True)
-        gram = jnp.einsum("ck,cl->kl", factor, factor, preferred_element_type=f32)
-        seen = jnp.dot(samples, factor, preferred_element_type=f32)
-        both = lax.psum(jnp.concatenate([gram, seen], axis=0), "chan")
+        both = lax.psum(exchange(local_factor.astype(jnp.bfloat16), samples, devices), "chan")
         coords, weights, weighted = fit(channels, both, sketched, norms)
     return (coords, weights[:, 0])
 
@@ -103,7 +226,7 @@
     out_specs = (P("tm", None), P("tm"))
 
     def whole(samples, sketch):
-        f = lambda a, b: shards(a, b, samples.shape[1])
+        f = lambda a, b: shards(a, b, samples.shape[1], mesh.shape["tm"])
         return jax.shard_map(f, mesh=mesh, in_specs=in_specs, out_specs=out_specs, check_vma=False)(samples, sketch)
 
     return whole

time: 632 us -> 573 us (0.907)
  waiting for transfers between devices: 469 us -> 143 us
  Pallas kernels: 98.6 us -> 365 us
  local copies, waits for them, and re-layouts: 3.74 us -> 25.4 us
  matrix products: 34.5 us -> 17.8 us
    pallas_call x0 -> x2, Pallas kernels: none -> 266 us  [exchange(): pl.pallas_call(functools.partial(exchange_kernel, outer, inner), out_shap...]
    reduce_scatter x2 -> x0, waiting for transfers between devices: 177 us -> none  [shards(): lax.psum_scatter(local_factor.astype(jnp.bfloat16), 'tm', scatter_dimensi...]
    all_gather x2 -> x0, waiting for transfers between devices: 152 us -> none  [shards(): factor = lax.all_gather(part, 'tm', axis=0, tiled=True)]
    dot_general x4 -> x0, matrix products: 16.6 us -> none  [the longest x2 11.9 us: shards(): seen = jnp.dot(samples, factor, preferred_element_type=f32)]
    convert_element_type x0 -> x2, local copies, waits for them, and re-layouts: none -> 13 us  [shards(): local_factor.astype(jnp.bfloat16)]
    unnamed x12 -> x16, local copies, waits for them, and re-layouts: 3.48 us -> 12.1 us
  transfers between devices with their start and end apart: 7 -> 3, of which waited for: 7 -> 3; matrix products, arithmetic and copies ran while one was open for 0% -> 0% of each run, Pallas kernels for 0% -> 0%
where the time goes in v3:
time: 573 us; the launch traced here: 570 us
  Pallas kernels  365 us (64%)
  waiting for transfers between devices  143 us (25%)
  local copies, waits for them, and re-layouts  25.4 us (4%)
  matrix products  17.8 us (3%)
  between operations  13.8 us (2%)
    pallas_call x2, Pallas kernels, exchange(): pl.pallas_call(functools.partial(exchange_kernel, outer, inner), out_shap...  266 us
    psum x2, waiting for transfers between devices, shards(): lax.psum(exchange(local_factor.astype(jnp.bfloat16), samples, devices), '...  103 us
    pallas_call x2, Pallas kernels, fit(): pl.pallas_call(functools.partial(fit_kernel, channels), out_shape=(jax.Sh...  98.6 us
    psum x1, waiting for transfers between devices, shards(): both = lax.psum(both, 'chan')  39.2 us
    dot_general x2, matrix products, shards(): jnp.einsum('sc,sk->ck', samples, weighted, preferred_element_type=f32)  13.3 us
    convert_element_type x2, local copies, waits for them, and re-layouts, shards(): local_factor.astype(jnp.bfloat16)  13 us
    unnamed x16, local copies, waits for them, and re-layouts  12.1 us
  transfers between devices with their start and end apart: 3, of which 3 were waited for; matrix products, arithmetic and copies ran while one was open for 0% of the time, Pallas kernels for 0%

profile of v3, /device:TPU:29, one launch (start us, length us, event | category | flops | bytes accessed | tf_op | source)
XLA Modules:
  0.0 569.7 jit_solution(6768068787032174256)
XLA Ops:
  7.2 0.0 all-reduce.4.cloned.1.call-start
  7.2 0.0 copy-start
  7.2 3.2 multiply_reduce_fusion
  10.5 0.2 copy-done
  10.7 4.5 fusion.4
  15.2 0.1 broadcast_in_dim.2
  15.3 1.2 pad_maximum_fusion
  16.5 0.0 all-reduce.4.cloned.1.call-update
  16.5 0.0 all-reduce.6.cloned.1.call-start
  16.6 39.2 %all-reduce.4.cloned.1.call-done = f32[512,640]{1,0:T(8,128)} async-done(((f32[512,640]{1,0:T(8,128)}), f32[512,640]{1,0:T(8,128)}) %all-reduce.4.cloned.1.call-update) | async-done | bytes 1310736 | tf_op jit(solution)/shard_map/psum | solution.py:214
  55.8 6.8 %fusion = bf16[4096,512]{0,1:T(8,128)(2,1)} fusion(bf16[512,4096]{1,0:T(8,128)(2,1)} %samples_ref.3, f32[512,640]{1,0:T(8,128)} %all-reduce.4.cloned.1.call-done), kind=kOutput, calls=%fused_computation.3 | convolution fusion | flops 2149580800 | bytes 8912896 | tf_op jit(solution)/shard_map/sc,sk->ck/dot_general | solution.py:218
  62.6 6.5 %copy.8 = bf16[4096,512]{1,0:T(8,128)(2,1)} copy(bf16[4096,512]{0,1:T(8,128)(2,1)} %fusion) | data formatting | bytes 8388608 | tf_op jit(solution)/shard_map/convert_element_type | solution.py:219
  69.1 2.2 copy-done.1
  71.3 2.2 copy-done.3
  73.5 133.1 %shard_map.41 = f32[1024,512]{1,0:T(8,128)} custom-call(bf16[8,512,512]{2,1,0:T(8,128)(2,1)S(1)} %bitcast.11, bf16[512,4096]{1,0:T(8,128)(2,1)S(1)} %copy-done.1), custom_call_target="tpu_custom_call" | custom-call | tf_op jit(solution)/shard_map/pallas_call | solution.py:185
  206.6 0.0 all-reduce.6.cloned.1.call-update
  206.6 0.2 all-reduce.8.cloned.1.call-start
  206.9 0.0 copy-done.7
  206.9 0.1 slice.8.sketched_ref
  207.0 51.4 %all-reduce.6.cloned.1.call-done.both_ref = f32[1024,512]{1,0:T(8,128)} async-done(((f32[1024,512]{1,0:T(8,128)}), f32[1024,512]{1,0:T(8,128)}) %all-reduce.6.cloned.1.call-update) | async-done | bytes 2097168 | tf_op jit(solution)/shard_map/psum | solution.py:219
  258.5 1.6 copy-done.5
  260.1 49.2 %shard_map.42 = (f32[512,512]{1,0:T(8,128)}, f32[512,1]{1,0:T(8,128)}, bf16[512,512]{1,0:T(8,128)(2,1)S(1)}) custom-call(f32[1024,512]{1,0:T(8,128)S(1)} %copy-done.5, f32[512,512]{1,0:T(8,128)S(1)} %slice.8.sketched_ref, f32[512,128]{1,0:T(8,128)S(1)} %slice.9.norms_ref), custom_call_target="tpu_custom_call" | custom-call | tf_op jit(solution)/shard_map/pallas_call | solution.py:69
  309.3 6.5 %fusion.1 = bf16[4096,512]{0,1:T(8,128)(2,1)} fusion(bf16[512,512]{1,0:T(8,128)(2,1)S(1)} %get-tuple-element.5, bf16[512,4096]{1,0:T(8,128)(2,1)} %samples_ref.3), kind=kOutput, calls=%fused_computation.4 | convolution fusion | flops 2149580800 | bytes 8912896 | tf_op jit(solution)/shard_map/sc,sk->ck/dot_general | solution.py:218
  315.8 6.5 %copy.9 = bf16[4096,512]{1,0:T(8,128)(2,1)} copy(bf16[4096,512]{0,1:T(8,128)(2,1)} %fusion.1) | data formatting | bytes 8388608 | tf_op jit(solution)/shard_map/convert_element_type | solution.py:219
  322.3 2.2 copy-done.2
  324.5 2.2 copy-done.4
  326.7 133.0 %shard_map.43 = f32[1024,512]{1,0:T(8,128)} custom-call(bf16[8,512,512]{2,1,0:T(8,128)(2,1)S(1)} %bitcast.12, bf16[512,4096]{1,0:T(8,128)(2,1)S(1)} %copy-done.2), custom_call_target="tpu_custom_call" | custom-call | tf_op jit(solution)/shard_map/pallas_call | solution.py:185
  459.7 0.0 all-reduce.8.cloned.1.call-update
  459.7 51.8 %all-reduce.8.cloned.1.call-done.both_ref = f32[1024,512]{1,0:T(8,128)} async-done(((f32[1024,512]{1,0:T(8,128)}), f32[1024,512]{1,0:T(8,128)}) %all-reduce.8.cloned.1.call-update) | async-done | bytes 2097168 | tf_op jit(solution)/shard_map/psum | solution.py:219
  511.5 1.6 copy-done.6
  513.1 49.3 %shard_map.44 = (f32[512,512]{1,0:T(8,128)}, f32[512,1]{1,0:T(8,128)S(1)}, bf16[512,512]{1,0:T(8,128)(2,1)}) custom-call(f32[1024,512]{1,0:T(8,128)S(1)} %copy-done.6, f32[512,512]{1,0:T(8,128)S(1)} %slice.8.sketched_ref, f32[512,128]{1,0:T(8,128)S(1)} %slice.9.norms_ref), custom_call_target="tpu_custom_call" | custom-call | tf_op jit(solution)/shard_map/pallas_call | solution.py:69
  562.4 0.7 reduce
  (8 shorter events, 0.0 us)
Async XLA Ops:
  7.2 48.6 %all-reduce.4.cloned.1.call-start = ((), (), s32[]{:S(2)}) async-start(), calls=%async_computation | async-start | bytes 2621440 | tf_op jit(solution)/shard_map/psum | solution.py:214
  7.2 3.5 copy-start
  16.5 241.9 %all-reduce.6.cloned.1.call-start = ((), (), s32[]{:S(2)}) async-start(), calls=%async_computation.1 | async-start | bytes 4194304 | tf_op jit(solution)/shard_map/psum | solution.py:219
  69.1 2.2 copy-start.1
  71.3 2.2 copy-start.3
  73.5 133.3 %copy-start.7 = (f32[512,640]{1,0:T(8,128)S(1)}, f32[512,640]{1,0:T(8,128)}, u32[]{:S(2)}) copy-start(f32[512,640]{1,0:T(8,128)} %all-reduce.4.cloned.1.call-done) | copy-start | bytes 3932164
  206.6 304.9 %all-reduce.8.cloned.1.call-start = ((), (), s32[]{:S(2)}) async-start(), calls=%async_computation.2 | async-start | bytes 4194304 | tf_op jit(solution)/shard_map/psum | solution.py:219
  258.5 1.6 copy-start.5
  322.3 2.2 copy-start.2
  324.5 2.2 copy-start.4
  511.5 1.6 copy-start.6
Sparse Core Ops, SparseCore 0:
  16.6 39.1 all-reduce.3
  206.7 51.6 all-reduce.5
  459.8 51.6 all-reduce.7

commit v4 on v3

--- a/solution.py
+++ b/solution.py
@@ -36,46 +36,175 @@
             right = right - col * row_right
 
 
-def fit_kernel(channels, both_ref, sketched_ref, norms_ref, coords_ref, weights_ref, weighted_ref, work, inv):
-    rank = coords_ref.shape[1]
-    total = work.shape[0]
-    work[...] = both_ref[...]
+def copier(sems, axis, count):
+    me = lax.axis_index(axis)
+
+    def copy(slot, d, src, dst):
+        return pltpu.make_async_remote_copy(
+            src_ref=src,
+            dst_ref=dst,
+            send_sem=sems.at[0, slot, d - 1],
+            recv_sem=sems.at[1, slot, d - 1],
+            device_id={axis: (me + d) % count},
+            device_id_type=MESH,
+        )
+
+    return copy
+
+
+def greet(axis, count):
+    me = lax.axis_index(axis)
+    barrier = pltpu.get_barrier_semaphore()
+    for d in range(1, count):
+        pl.semaphore_signal(barrier, inc=1, device_id={axis: (me + d) % count}, device_id_type=MESH)
+    pl.semaphore_wait(barrier, count - 1)
+
+
+def part(index, size, base=0):
+    return pl.ds(pl.multiple_of(base + index * size, size), size)
+
+
+def scatter_copies(copy, slot, count, source, base, size, slots):
+    me = lax.axis_index("chan")
+    return [
+        copy(slot, d, source.at[part((me + d) % count, size, base)], slots.at[d - 1]) for d in range(1, count)
+    ]
+
+
+def gather_rows(copy, slot, count, whole, size):
+    me = lax.axis_index("chan")
+    sends = [copy(slot, d, whole.at[part(me, size)], whole.at[part(me, size)]) for d in range(1, count)]
+    for one in sends:
+        one.start()
+    for d in range(1, count):
+        came = whole.at[part((me - d + count) % count, size)]
+        copy(slot, d, came, came).wait_recv()
+    for one in sends:
+        one.wait_send()
+
+
+def start_kernel(count, local_ref, own_ref, weighted_ref, slots, gathered, sems):
+    size, rank = slots.shape[1], weighted_ref.shape[1]
+    me = lax.axis_index("chan")
+    greet("chan", count)
+    copy = copier(sems, "chan", count)
+    sends = scatter_copies(copy, 0, count, local_ref, 0, size, slots)
+    for one in sends:
+        one.start()
+    total = local_ref[part(me, size)]
+    for one in sends:
+        one.wait_recv()
+    for d in range(1, count):
+        total = total + slots[d - 1]
+    own_ref[...] = total
+    gathered[part(me, size)] = total[:, :rank].astype(jnp.bfloat16)
+    gather_rows(copy, 1, count, gathered, size)
+    for one in sends:
+        one.wait_send()
+    weighted_ref[...] = gathered[...]
+
+
+def start(local, rank, count):
+    rows, wide = local.shape
+    size = rows // count
+    return pl.pallas_call(
+        functools.partial(start_kernel, count),
+        out_shape=(
+            jax.ShapeDtypeStruct((size, wide), jnp.float32),
+            jax.ShapeDtypeStruct((rows, rank), jnp.bfloat16),
+        ),
+        scratch_shapes=[
+            pltpu.VMEM((count - 1, size, wide), jnp.float32),
+            pltpu.VMEM((rows, rank), jnp.bfloat16),
+            pltpu.SemaphoreType.DMA((2, 2, count - 1)),
+        ],
+        compiler_params=pltpu.CompilerParams(
+            collective_id=1, has_side_effects=True, vmem_limit_bytes=32 * 1024 * 1024
+        ),
+    )(local)
+
+
+def fit_kernel(channels, count, last, both_ref, own_ref, out_ref, gram_slots, seen_slots, work, inv, gathered, sems):
+    rank = work.shape[0]
+    size, rows = gram_slots.shape[1], seen_slots.shape[1]
+    me = lax.axis_index("chan")
+    greet("chan", count)
+    copy = copier(sems, "chan", count)
+    grams = scatter_copies(copy, 0, count, both_ref, 0, size, gram_slots)
+    seens = scatter_copies(copy, 1, count, both_ref, rank, rows, seen_slots)
+    for one in grams:
+        one.start()
+    total = both_ref[part(me, size)]
+    for one in grams:
+        one.wait_recv()
+    for d in range(1, count):
+        total = total + gram_slots[d - 1]
+    work[part(me, size)] = total
+    gather_rows(copy, 2, count, work, size)
+    for one in seens:
+        one.start()
 
     def block_step(b, carry):
         at = pl.multiple_of(b * B, B)
-        invert_block(work[pl.ds(at, B), pl.ds(at, B)], inv)
-        for k in range(rank // B):
+        invert_block(work[pl.ds(at, B), pl.ds(at, B)], inv.at[b])
+        for k in range(rank // B - 1):
 
             @pl.when(b == k)
             def _():
                 lo, hi = k * B, (k + 1) * B
-                panel = dot_t(work[hi:, lo:hi], inv[...])
-                coords_ref[:, lo:hi] = panel[rank - hi :]
-                if hi < rank:
-                    work[hi:, hi:] = work[hi:, hi:] - dot_t(panel, panel[: rank - hi])
+                panel = dot_t(work[hi:, lo:hi], inv[k])
+                work[hi:, lo:hi] = panel
+                work[hi:, hi:] = work[hi:, hi:] - dot_t(panel, panel)
 
         return carry
 
     lax.fori_loop(0, rank // B, block_step, 0)
-    coords = coords_ref[...]
-    energy = jnp.maximum(norms_ref[:, :1] - jnp.sum(coords * coords, axis=1, keepdims=True), 0.0)
+    for one in seens:
+        one.wait_recv()
+    seen = both_ref[part(me, rows, rank)]
+    for d in range(1, count):
+        seen = seen + seen_slots[d - 1]
+    solved = []
+    for k in range(rank // B):
+        lo, hi = k * B, (k + 1) * B
+        rest = seen[:, lo:hi]
+        if k:
+            rest = rest - dot_t(jnp.concatenate(solved, axis=1), work[lo:hi, :lo])
+        solved.append(dot_t(rest, inv[k]))
+    coords = jnp.concatenate(solved, axis=1)
+    own = own_ref[...]
+    energy = jnp.maximum(own[:, rank : rank + 1] - jnp.sum(coords * coords, axis=1, keepdims=True), 0.0)
     weights = jnp.minimum(1.0, 3.0 / jnp.sqrt(energy / channels + 1e-06))
-    weights_ref[...] = weights
-    weighted_ref[...] = ((weights * weights) * sketched_ref[...]).astype(jnp.bfloat16)
-
-
-def fit(channels, both, sketched, norms):
-    rows, rank = sketched.shape
+    if last:
+        gathered[part(me, rows), :rank] = coords
+        gathered[part(me, rows), rank:] = jnp.broadcast_to(weights, (rows, B))
+    else:
+        gathered[part(me, rows)] = ((weights * weights) * own[:, :rank]).astype(jnp.bfloat16)
+    gather_rows(copy, 3, count, gathered, rows)
+    for one in grams + seens:
+        one.wait_send()
+    out_ref[...] = gathered[...]
+
+
+def fit(channels, count, last, both, own):
+    size, rank = own.shape[0], both.shape[1]
+    rows = size * count
+    kept = ((rows, rank + B), jnp.float32) if last else ((rows, rank), jnp.bfloat16)
     return pl.pallas_call(
-        functools.partial(fit_kernel, channels),
-        out_shape=(
-            jax.ShapeDtypeStruct((rows, rank), jnp.float32),
-            jax.ShapeDtypeStruct((rows, 1), jnp.float32),
-            jax.ShapeDtypeStruct((rows, rank), jnp.bfloat16),
+        functools.partial(fit_kernel, channels, count, last),
+        out_shape=jax.ShapeDtypeStruct(*kept),
+        scratch_shapes=[
+            pltpu.VMEM((count - 1, rank // count, rank), jnp.float32),
+            pltpu.VMEM((count - 1, size, rank), jnp.float32),
+            pltpu.VMEM((rank, rank), jnp.float32),
+            pltpu.VMEM((rank // B, B, B), jnp.float32),
+            pltpu.VMEM(*kept),
+            pltpu.SemaphoreType.DMA((2, 4, count - 1)),
+        ],
+        compiler_params=pltpu.CompilerParams(
+            collective_id=3 if last else 2, has_side_effects=True, vmem_limit_bytes=32 * 1024 * 1024
         ),
-        scratch_shapes=[pltpu.VMEM(both.shape, jnp.float32), pltpu.VMEM((B, B), jnp.float32)],
-        compiler_params=pltpu.CompilerParams(vmem_limit_bytes=32 * 1024 * 1024),
-    )(both, sketched, norms)
+    )(both, own)
 
 
 def exchange_kernel(outer, inner, mine_ref, samples_ref, both_ref, whole, near, sent, far, acc, near_sem, far_sem, wide_sem, local_sem):
@@ -147,10 +276,10 @@
     both_ref[...] = jnp.zeros_like(both_ref)
 
     def use(block):
-        part = whole[block]
+        one = whole[block]
         columns = pl.ds(pl.multiple_of(block * size, size), size)
-        both_ref[:rank] += lax.dot_general(part, part, (((0,), (0,)), ((), ())), preferred_element_type=f32)
-        both_ref[rank:] += jnp.dot(samples_ref[:, columns], part, preferred_element_type=f32)
+        both_ref[:rank] += lax.dot_general(one, one, (((0,), (0,)), ((), ())), preferred_element_type=f32)
+        both_ref[rank:] += jnp.dot(samples_ref[:, columns], one, preferred_element_type=f32)
 
     use(me)
     for e in range(1, outer):
@@ -204,21 +333,19 @@
     )(mine.reshape(devices, size, rank), samples)
 
 
-def shards(samples, sketch, channels, devices):
+def shards(samples, sketch, channels, devices, count):
     rows, rank = samples.shape[0], sketch.shape[1]
     f32 = jnp.float32
     wide = samples.astype(f32)
     norms = jnp.sum(wide * wide, axis=1)
     local = jnp.dot(samples, sketch, preferred_element_type=f32)
-    both = jnp.concatenate([local, jnp.broadcast_to(norms[:, None], (rows, 128))], axis=1)
-    both = lax.psum(both, "chan")
-    sketched, norms = both[:, :rank], both[:, rank:]
-    weighted = sketched.astype(jnp.bfloat16)
+    local = jnp.concatenate([local, jnp.broadcast_to(norms[:, None], (rows, B))], axis=1)
+    own, weighted = start(local, rank, count)
     for step in range(ROUNDS):
         local_factor = jnp.einsum("sc,sk->ck", samples, weighted, preferred_element_type=f32)
-        both = lax.psum(exchange(local_factor.astype(jnp.bfloat16), samples, devices), "chan")
-        coords, weights, weighted = fit(channels, both, sketched, norms)
-    return (coords, weights[:, 0])
+        both = exchange(local_factor.astype(jnp.bfloat16), samples, devices)
+        weighted = fit(channels, count, step == ROUNDS - 1, both, own)
+    return (weighted[:, :rank], weighted[:, rank])
 
 
 def solution(mesh):
@@ -226,7 +353,7 @@
     out_specs = (P("tm", None), P("tm"))
 
     def whole(samples, sketch):
-        f = lambda a, b: shards(a, b, samples.shape[1], mesh.shape["tm"])
+        f = lambda a, b: shards(a, b, samples.shape[1], mesh.shape["tm"], mesh.shape["chan"])
         return jax.shard_map(f, mesh=mesh, in_specs=in_specs, out_specs=out_specs, check_vma=False)(samples, sketch)
 
     return whole

time: 573 us -> 497 us (0.87)
  waiting for transfers between devices: 143 us -> 0 us
  Pallas kernels: 365 us -> 455 us
  between operations: 13.8 us -> 0.7 us
    psum x3 -> x0, waiting for transfers between devices: 143 us -> none  [the longest x2 103 us: shards(): lax.psum(exchange(local_factor.astype(jnp.bfloat16), samples, devices), '...]
    pallas_call x2 -> x3, Pallas kernels: 98.6 us -> 190 us  [the longest x2 167 us: fit(): pl.pallas_call(functools.partial(fit_kernel, channels, count, last), out_...]
    unnamed x16 -> x10, local copies, waits for them, and re-layouts: 12.1 us -> 8.83 us
  transfers between devices with their start and end apart: 3 -> 0, of which waited for: 3 -> 0; matrix products, arithmetic and copies ran while one was open for 0% -> 0% of each run, Pallas kernels for 0% -> 0%
where the time goes in v4:
time: 497 us; the launch traced here: 496 us
  Pallas kernels  455 us (92%)
  local copies, waits for them, and re-layouts  23.9 us (5%)
  matrix products  13.1 us (3%)
    pallas_call x2, Pallas kernels, exchange(): pl.pallas_call(functools.partial(exchange_kernel, outer, inner), out_shap...  266 us
    pallas_call x2, Pallas kernels, fit(): pl.pallas_call(functools.partial(fit_kernel, channels, count, last), out_...  167 us
    pallas_call x1, Pallas kernels, start(): pl.pallas_call(functools.partial(start_kernel, count), out_shape=(jax.Sha...  22.9 us
    convert_element_type x2, local copies, waits for them, and re-layouts, shards(): both = exchange(local_factor.astype(jnp.bfloat16), samples, devices)  13.1 us

profile of v4, /device:TPU:29, one launch (start us, length us, event | category | flops | bytes accessed | tf_op | source)
XLA Modules:
  0.0 496.4 jit_solution(16909149667877694430)
XLA Ops:
  0.6 0.0 copy-start
  0.6 3.2 multiply_reduce_fusion
  3.9 0.1 broadcast_in_dim.2
  4.0 0.1 copy-done
  4.1 4.5 fusion.2
  8.6 0.1 pad_maximum_fusion.local_ref
  8.7 22.9 %shard_map.41 = (f32[128,640]{1,0:T(8,128)S(1)}, bf16[512,512]{1,0:T(8,128)(2,1)S(1)}) custom-call(f32[512,640]{1,0:T(8,128)S(1)} %pad_maximum_fusion.local_ref), custom_call_target="tpu_custom_call" | custom-call | tf_op jit(solution)/shard_map/pallas_call | solution.py:110
  31.6 4.3 fusion
  35.9 6.5 %copy.8 = bf16[4096,512]{1,0:T(8,128)(2,1)} copy(bf16[4096,512]{0,1:T(8,128)(2,1)} %fusion) | data formatting | bytes 8388608 | tf_op jit(solution)/shard_map/convert_element_type | solution.py:346
  42.4 0.0 copy-start.1
  42.4 2.2 copy-done.1
  44.6 0.0 copy-start.3
  44.6 2.2 copy-done.3
  46.8 133.2 %shard_map.42.both_ref = f32[1024,512]{1,0:T(8,128)S(1)} custom-call(bf16[8,512,512]{2,1,0:T(8,128)(2,1)S(1)} %bitcast.12, bf16[512,4096]{1,0:T(8,128)(2,1)S(1)} %copy-done.1), custom_call_target="tpu_custom_call" | custom-call | tf_op jit(solution)/shard_map/pallas_call | solution.py:314
  180.1 79.3 %shard_map.43 = bf16[512,512]{1,0:T(8,128)(2,1)S(1)} custom-call(f32[1024,512]{1,0:T(8,128)S(1)} %shard_map.42.both_ref, f32[128,640]{1,0:T(8,128)S(1)} %get-tuple-element.5.own_ref), custom_call_target="tpu_custom_call" | custom-call | tf_op jit(solution)/shard_map/pallas_call | solution.py:193
  259.3 4.3 fusion.1
  263.6 6.5 %copy.9 = bf16[4096,512]{1,0:T(8,128)(2,1)} copy(bf16[4096,512]{0,1:T(8,128)(2,1)} %fusion.1) | data formatting | bytes 8388608 | tf_op jit(solution)/shard_map/convert_element_type | solution.py:346
  270.2 0.0 copy-start.2
  270.2 2.2 copy-done.2
  272.4 0.0 copy-start.4
  272.4 2.2 copy-done.4
  274.5 132.4 %shard_map.44.both_ref = f32[1024,512]{1,0:T(8,128)S(1)} custom-call(bf16[8,512,512]{2,1,0:T(8,128)(2,1)S(1)} %bitcast.13, bf16[512,4096]{1,0:T(8,128)(2,1)S(1)} %copy-done.2), custom_call_target="tpu_custom_call" | custom-call | tf_op jit(solution)/shard_map/pallas_call | solution.py:314
  406.9 87.6 %shard_map.45 = f32[512,640]{1,0:T(8,128)S(1)} custom-call(f32[1024,512]{1,0:T(8,128)S(1)} %shard_map.44.both_ref, f32[128,640]{1,0:T(8,128)S(1)} %get-tuple-element.5.own_ref), custom_call_target="tpu_custom_call" | custom-call | tf_op jit(solution)/shard_map/pallas_call | solution.py:193
  494.5 0.7 slice_reduce_fusion
  495.2 1.1 slice.6
Async XLA Ops:
  0.6 3.5 copy-start
  42.4 2.2 copy-start.1
  44.6 2.2 copy-start.3
  270.2 2.2 copy-start.2
  272.4 2.2 copy-start.4

commit v5 on v4

--- a/solution.py
+++ b/solution.py
@@ -9,6 +9,7 @@
 
 ROUNDS = 2
 B = 128
+GROUP = 4
 HIGH = lax.Precision.HIGHEST
 MESH = pl.DeviceIdType.MESH
 
@@ -21,19 +22,35 @@
     eye = lax.broadcasted_iota(jnp.int32, (B, B), 0) == lax.broadcasted_iota(jnp.int32, (B, B), 1)
     left, right = block, eye.astype(jnp.float32)
     top = 0
-    for j in range(B):
+    for j in range(0, B, GROUP):
         cut = (j // 8) * 8 - top
         if cut:
             left, right, top = left[cut:], right[cut:], top + cut
         k = j - top
-        scale = lax.rsqrt(left[k : k + 1, j : j + 1])
-        row_left = left[k : k + 1, :] * scale
-        row_right = right[k : k + 1, :] * scale
-        inv_ref[j : j + 1, :] = row_right
-        if j + 1 < B:
-            col = left[:, j : j + 1] * scale
-            left = left - col * row_left
-            right = right - col * row_right
+        span = range(GROUP)
+        rows = [left[k + t : k + t + 1, :] for t in span]
+        rights = [right[k + t : k + t + 1, :] for t in span]
+        cols = [jnp.broadcast_to(left[:, j + t : j + t + 1], left.shape) for t in span]
+        pivot = {
+            (u, t): jnp.broadcast_to(left[k + u : k + u + 1, j + t : j + t + 1], (1, B))
+            for u in span
+            for t in range(u + 1)
+        }
+        for t in span:
+            scale = lax.rsqrt(pivot[t, t])
+            rows[t], rights[t], cols[t] = rows[t] * scale, rights[t] * scale, cols[t] * scale
+            below = {u: pivot[u, t] * scale for u in range(t + 1, GROUP)}
+            for u in below:
+                rows[u] = rows[u] - below[u] * rows[t]
+                rights[u] = rights[u] - below[u] * rights[t]
+                cols[u] = cols[u] - below[u] * cols[t]
+                for v in range(t + 1, u + 1):
+                    pivot[u, v] = pivot[u, v] - below[u] * below[v]
+            inv_ref[j + t : j + t + 1, :] = rights[t]
+        if j + GROUP < B:
+            for t in span:
+                left = left - cols[t] * rows[t]
+                right = right - cols[t] * rights[t]
 
 
 def copier(sems, axis, count):
@@ -207,7 +224,7 @@
     )(both, own)
 
 
-def exchange_kernel(outer, inner, mine_ref, samples_ref, both_ref, whole, near, sent, far, acc, near_sem, far_sem, wide_sem, local_sem):
+def exchange_kernel(outer, inner, weighted_ref, samples_ref, both_ref, mine_ref, whole, near, sent, far, acc, near_sem, far_sem, wide_sem, local_sem):
     me = lax.axis_index("tm")
     o, i = me // inner, me % inner
     size, rank = acc.shape
@@ -236,19 +253,26 @@
             device_id_type=MESH,
         )
 
+    def factor(block):
+        columns = pl.ds(pl.multiple_of(block * size, size), size)
+        return lax.dot_general(
+            samples_ref[:, columns], weighted_ref[...], (((0,), (0,)), ((), ())), preferred_element_type=f32
+        )
+
     order = list(range(1, outer)) + [0]
     first = {}
     for e in order:
         row = (o + e) % outer
         for d in range(1, inner):
             block = row * inner + (i + d) % inner
+            mine_ref[block] = factor(block).astype(jnp.bfloat16)
             first[e, d] = copy(mine_ref.at[block], near.at[e, d - 1], near_sem, (e, d - 1), peer_in(d))
             first[e, d].start()
     second = {}
     for e in order:
+        total = factor(((o + e) % outer) * inner + i)
         for d in range(1, inner):
             first[e, d].wait_recv()
-        total = mine_ref[((o + e) % outer) * inner + i].astype(f32)
         for d in range(1, inner):
             total = total + near[e, d - 1].astype(f32)
         if e:
@@ -304,9 +328,9 @@
             local(e, d).wait_send()
 
 
-def exchange(mine, samples, devices):
+def exchange(weighted, samples, devices):
     rows, channels = samples.shape
-    rank = mine.shape[1]
+    rank = weighted.shape[1]
     outer = 4 if devices % 4 == 0 else 1
     inner = devices // outer
     size = channels // devices
@@ -317,6 +341,7 @@
         in_specs=[pl.BlockSpec(memory_space=pltpu.VMEM)] * 2,
         out_specs=pl.BlockSpec(memory_space=pltpu.VMEM),
         scratch_shapes=[
+            pltpu.VMEM((devices, size, rank), low),
             pltpu.VMEM((devices, size, rank), low),
             pltpu.VMEM((outer, inner - 1, size, rank), low),
             pltpu.VMEM((outer - 1, size, rank), low),
@@ -330,7 +355,7 @@
         compiler_params=pltpu.CompilerParams(
             collective_id=0, has_side_effects=True, vmem_limit_bytes=40 * 1024 * 1024
         ),
-    )(mine.reshape(devices, size, rank), samples)
+    )(weighted, samples)
 
 
 def shards(samples, sketch, channels, devices, count):
@@ -342,8 +367,7 @@
     local = jnp.concatenate([local, jnp.broadcast_to(norms[:, None], (rows, B))], axis=1)
     own, weighted = start(local, rank, count)
     for step in range(ROUNDS):
-        local_factor = jnp.einsum("sc,sk->ck", samples, weighted, preferred_element_type=f32)
-        both = exchange(local_factor.astype(jnp.bfloat16), samples, devices)
+        both = exchange(weighted, samples, devices)
         weighted = fit(channels, count, step == ROUNDS - 1, both, own)
     return (weighted[:, :rank], weighted[:, rank])
 

time: 497 us -> 416 us (0.84)
  Pallas kernels: 455 us -> 405 us
  local copies, waits for them, and re-layouts: 23.9 us -> 2.04 us
  matrix products: 13.1 us -> 4.51 us
    pallas_call x2, Pallas kernels: 167 us -> 115 us  [fit(): pl.pallas_call(functools.partial(fit_kernel, channels, count, last), out_...]
    convert_element_type x2 -> x0, local copies, waits for them, and re-layouts: 13.1 us -> none  [shards(): both = exchange(local_factor.astype(jnp.bfloat16), samples, devices)]
    unnamed x10 -> x2, local copies, waits for them, and re-layouts: 8.83 us -> 0.08 us
    dot_general x2 -> x0, matrix products: 8.62 us -> none  [shards(): jnp.einsum('sc,sk->ck', samples, weighted, preferred_element_type=f32)]
where the time goes in v5:
time: 416 us
  Pallas kernels  405 us (97%)
  matrix products  4.51 us (1%)
    pallas_call x2, Pallas kernels, exchange(): pl.pallas_call(functools.partial(exchange_kernel, outer, inner), out_shap...  267 us
    pallas_call x2, Pallas kernels, fit(): pl.pallas_call(functools.partial(fit_kernel, channels, count, last), out_...  115 us
    pallas_call x1, Pallas kernels, start(): pl.pallas_call(functools.partial(start_kernel, count), out_shape=(jax.Sha...  22.9 us

profile of v5, /device:TPU:29, one launch (start us, length us, event | category | flops | bytes accessed | tf_op | source)
XLA Modules:
  0.0 416.0 jit_solution(7570225667746612158)
XLA Ops:
  0.6 0.0 copy-start
  0.6 3.2 multiply_reduce_fusion
  3.9 0.1 broadcast_in_dim.2
  4.0 0.1 copy-done
  4.1 4.5 %fusion = f32[512,512]{1,0:T(8,128)S(1)} fusion(bf16[512,4096]{1,0:T(8,128)(2,1)S(1)} %copy-done, bf16[4096,512]{1,0:T(8,128)(2,1)} %param.3), kind=kOutput, calls=%fused_computation.3 | convolution fusion | flops 2147483648 | bytes 9437184 | tf_op jit(solution)/shard_map/dot_general | solution.py:366
  8.6 0.1 pad_maximum_fusion.local_ref
  8.7 22.9 %shard_map.41 = (f32[128,640]{1,0:T(8,128)S(1)}, bf16[512,512]{1,0:T(8,128)(2,1)S(1)}) custom-call(f32[512,640]{1,0:T(8,128)S(1)} %pad_maximum_fusion.local_ref), custom_call_target="tpu_custom_call" | custom-call | tf_op jit(solution)/shard_map/pallas_call | solution.py:127
  31.6 134.1 %shard_map.42.both_ref = f32[1024,512]{1,0:T(8,128)S(1)} custom-call(bf16[512,512]{1,0:T(8,128)(2,1)S(1)} %get-tuple-element.4.weighted_ref, bf16[512,4096]{1,0:T(8,128)(2,1)S(1)} %copy-done), custom_call_target="tpu_custom_call" | custom-call | tf_op jit(solution)/shard_map/pallas_call | solution.py:338
  165.7 53.4 %shard_map.43.weighted_ref = bf16[512,512]{1,0:T(8,128)(2,1)S(1)} custom-call(f32[1024,512]{1,0:T(8,128)S(1)} %shard_map.42.both_ref, f32[128,640]{1,0:T(8,128)S(1)} %get-tuple-element.5.own_ref), custom_call_target="tpu_custom_call" | custom-call | tf_op jit(solution)/shard_map/pallas_call | solution.py:210
  219.1 133.2 %shard_map.44.both_ref = f32[1024,512]{1,0:T(8,128)S(1)} custom-call(bf16[512,512]{1,0:T(8,128)(2,1)S(1)} %shard_map.43.weighted_ref, bf16[512,4096]{1,0:T(8,128)(2,1)S(1)} %copy-done), custom_call_target="tpu_custom_call" | custom-call | tf_op jit(solution)/shard_map/pallas_call | solution.py:338
  352.4 61.8 %shard_map.45 = f32[512,640]{1,0:T(8,128)S(1)} custom-call(f32[1024,512]{1,0:T(8,128)S(1)} %shard_map.44.both_ref, f32[128,640]{1,0:T(8,128)S(1)} %get-tuple-element.5.own_ref), custom_call_target="tpu_custom_call" | custom-call | tf_op jit(solution)/shard_map/pallas_call | solution.py:210
  414.2 0.7 slice_reduce_fusion
  414.9 1.1 slice.6
Async XLA Ops:
  0.6 3.5 copy-start

commit v6 on v5

--- a/solution.py
+++ b/solution.py
@@ -10,6 +10,7 @@
 ROUNDS = 2
 B = 128
 GROUP = 4
+PIECES = 4
 HIGH = lax.Precision.HIGHEST
 MESH = pl.DeviceIdType.MESH
 
@@ -260,19 +261,23 @@
         )
 
     order = list(range(1, outer)) + [0]
-    first = {}
-    for e in order:
-        row = (o + e) % outer
+    first, second = {}, {}
+
+    def begin(e):
         for d in range(1, inner):
-            block = row * inner + (i + d) % inner
+            block = ((o + e) % outer) * inner + (i + d) % inner
             mine_ref[block] = factor(block).astype(jnp.bfloat16)
             first[e, d] = copy(mine_ref.at[block], near.at[e, d - 1], near_sem, (e, d - 1), peer_in(d))
             first[e, d].start()
-    second = {}
-    for e in order:
+
+    for e in order[:2]:
+        begin(e)
+    for at, e in enumerate(order):
         total = factor(((o + e) % outer) * inner + i)
         for d in range(1, inner):
             first[e, d].wait_recv()
+        for later in order[at + 2 : at + 3]:
+            begin(later)
         for d in range(1, inner):
             total = total + near[e, d - 1].astype(f32)
         if e:
@@ -286,17 +291,24 @@
         acc[...] = acc[...] + far[e - 1].astype(f32)
     whole[me] = acc[...].astype(jnp.bfloat16)
 
-    def wide(e):
-        return copy(whole.at[me], whole.at[me], wide_sem, (e - 1,), peer_out(e))
-
-    def local(e, d):
-        block = ((o - e + outer) % outer) * inner + i
-        return copy(whole.at[block], whole.at[block], local_sem, (e, d - 1), peer_in(d))
-
-    for e in range(1, outer):
-        wide(e).start()
-    for d in range(1, inner):
-        local(0, d).start()
+    step = size // PIECES
+
+    def piece(block, h):
+        return whole.at[block, pl.ds(h * step, step)]
+
+    def wide(e, h, block=me):
+        return copy(piece(block, h), piece(block, h), wide_sem, (e - 1, h), peer_out(e))
+
+    def local(e, d, h, shift=0):
+        block = ((o - e + outer) % outer) * inner + (i - shift + inner) % inner
+        return copy(piece(block, h), piece(block, h), local_sem, (e, d - 1, h), peer_in(d))
+
+    for h in range(2):
+        for e in range(1, outer):
+            wide(e, h).start()
+    for h in range(PIECES):
+        for d in range(1, inner):
+            local(0, d, h).start()
     both_ref[...] = jnp.zeros_like(both_ref)
 
     def use(block):
@@ -306,26 +318,31 @@
         both_ref[rank:] += jnp.dot(samples_ref[:, columns], one, preferred_element_type=f32)
 
     use(me)
+    for h in range(PIECES):
+        for e in range(1, outer):
+            block = ((o - e + outer) % outer) * inner + i
+            wide(e, h, block).wait_recv()
+            if h + 2 < PIECES:
+                wide(e, h + 2).start()
+            for d in range(1, inner):
+                local(e, d, h).start()
     for e in range(1, outer):
-        block = ((o - e + outer) % outer) * inner + i
-        copy(whole.at[block], whole.at[block], wide_sem, (e - 1,), peer_out(e)).wait_recv()
-        for d in range(1, inner):
-            local(e, d).start()
-        use(block)
+        use(((o - e + outer) % outer) * inner + i)
     for e in range(outer):
         for d in range(1, inner):
-            block = ((o - e + outer) % outer) * inner + (i - d + inner) % inner
-            copy(whole.at[block], whole.at[block], local_sem, (e, d - 1), peer_in(d)).wait_recv()
-            use(block)
+            for h in range(PIECES):
+                local(e, d, h, d).wait_recv()
+            use(((o - e + outer) % outer) * inner + (i - d + inner) % inner)
     for one in first.values():
         one.wait_send()
     for one in second.values():
         one.wait_send()
-    for e in range(1, outer):
-        wide(e).wait_send()
-    for e in range(outer):
-        for d in range(1, inner):
-            local(e, d).wait_send()
+    for h in range(PIECES):
+        for e in range(1, outer):
+            wide(e, h).wait_send()
+        for e in range(outer):
+            for d in range(1, inner):
+                local(e, d, h).wait_send()
 
 
 def exchange(weighted, samples, devices):
@@ -349,8 +366,8 @@
             pltpu.VMEM((size, rank), jnp.float32),
             pltpu.SemaphoreType.DMA((2, outer, inner - 1)),
             pltpu.SemaphoreType.DMA((2, outer - 1)),
-            pltpu.SemaphoreType.DMA((2, outer - 1)),
-            pltpu.SemaphoreType.DMA((2, outer, inner - 1)),
+            pltpu.SemaphoreType.DMA((2, outer - 1, PIECES)),
+            pltpu.SemaphoreType.DMA((2, outer, inner - 1, PIECES)),
         ],
         compiler_params=pltpu.CompilerParams(
             collective_id=0, has_side_effects=True, vmem_limit_bytes=40 * 1024 * 1024

time: 416 us -> 390 us (0.938)
  Pallas kernels: 405 us -> 379 us
    pallas_call x2, Pallas kernels: 267 us -> 240 us  [exchange(): pl.pallas_call(functools.partial(exchange_kernel, outer, inner), out_shap...]
where the time goes in v6:
time: 390 us
  Pallas kernels  379 us (97%)
  matrix products  4.51 us (1%)
    pallas_call x2, Pallas kernels, exchange(): pl.pallas_call(functools.partial(exchange_kernel, outer, inner), out_shap...  240 us
    pallas_call x2, Pallas kernels, fit(): pl.pallas_call(functools.partial(fit_kernel, channels, count, last), out_...  116 us
    pallas_call x1, Pallas kernels, start(): pl.pallas_call(functools.partial(start_kernel, count), out_shape=(jax.Sha...  22.9 us

profile of v6, /device:TPU:29, one launch (start us, length us, event | category | flops | bytes accessed | tf_op | source)
XLA Modules:
  0.0 389.5 jit_solution(726104942863942557)
XLA Ops:
  0.6 0.0 copy-start
  0.6 3.2 multiply_reduce_fusion
  3.9 0.1 broadcast_in_dim.2
  4.0 0.1 copy-done
  4.1 4.5 %fusion = f32[512,512]{1,0:T(8,128)S(1)} fusion(bf16[512,4096]{1,0:T(8,128)(2,1)S(1)} %copy-done, bf16[4096,512]{1,0:T(8,128)(2,1)} %param.3), kind=kOutput, calls=%fused_computation.3 | convolution fusion | flops 2147483648 | bytes 9437184 | tf_op jit(solution)/shard_map/dot_general | solution.py:383
  8.6 0.1 pad_maximum_fusion.local_ref
  8.7 22.9 %shard_map.41 = (f32[128,640]{1,0:T(8,128)S(1)}, bf16[512,512]{1,0:T(8,128)(2,1)S(1)}) custom-call(f32[512,640]{1,0:T(8,128)S(1)} %pad_maximum_fusion.local_ref), custom_call_target="tpu_custom_call" | custom-call | tf_op jit(solution)/shard_map/pallas_call | solution.py:128
  31.6 120.7 %shard_map.42.both_ref = f32[1024,512]{1,0:T(8,128)S(1)} custom-call(bf16[512,512]{1,0:T(8,128)(2,1)S(1)} %get-tuple-element.4.weighted_ref, bf16[512,4096]{1,0:T(8,128)(2,1)S(1)} %copy-done), custom_call_target="tpu_custom_call" | custom-call | tf_op jit(solution)/shard_map/pallas_call | solution.py:355
  152.3 53.8 %shard_map.43.weighted_ref = bf16[512,512]{1,0:T(8,128)(2,1)S(1)} custom-call(f32[1024,512]{1,0:T(8,128)S(1)} %shard_map.42.both_ref, f32[128,640]{1,0:T(8,128)S(1)} %get-tuple-element.5.own_ref), custom_call_target="tpu_custom_call" | custom-call | tf_op jit(solution)/shard_map/pallas_call | solution.py:211
  206.0 119.3 %shard_map.44.both_ref = f32[1024,512]{1,0:T(8,128)S(1)} custom-call(bf16[512,512]{1,0:T(8,128)(2,1)S(1)} %shard_map.43.weighted_ref, bf16[512,4096]{1,0:T(8,128)(2,1)S(1)} %copy-done), custom_call_target="tpu_custom_call" | custom-call | tf_op jit(solution)/shard_map/pallas_call | solution.py:355
  325.3 62.4 %shard_map.45 = f32[512,640]{1,0:T(8,128)S(1)} custom-call(f32[1024,512]{1,0:T(8,128)S(1)} %shard_map.44.both_ref, f32[128,640]{1,0:T(8,128)S(1)} %get-tuple-element.5.own_ref), custom_call_target="tpu_custom_call" | custom-call | tf_op jit(solution)/shard_map/pallas_call | solution.py:211
  387.7 0.7 slice_reduce_fusion
  388.4 1.1 slice.6
Async XLA Ops:
  0.6 3.5 copy-start

commit v7 on v6

--- a/solution.py
+++ b/solution.py
@@ -10,7 +10,7 @@
 ROUNDS = 2
 B = 128
 GROUP = 4
-PIECES = 4
+PIECES = 8
 HIGH = lax.Precision.HIGHEST
 MESH = pl.DeviceIdType.MESH
 

time: 390 us -> 387 us (level)
  no operation moved by 1% of the time
where the time goes in v7:
time: 387 us; the launch traced here: 386 us
  Pallas kernels  376 us (97%)
  matrix products  4.51 us (1%)
    pallas_call x2, Pallas kernels, exchange(): pl.pallas_call(functools.partial(exchange_kernel, outer, inner), out_shap...  237 us
    pallas_call x2, Pallas kernels, fit(): pl.pallas_call(functools.partial(fit_kernel, channels, count, last), out_...  115 us
    pallas_call x1, Pallas kernels, start(): pl.pallas_call(functools.partial(start_kernel, count), out_shape=(jax.Sha...  22.9 us

profile of v7, /device:TPU:29, one launch (start us, length us, event | category | flops | bytes accessed | tf_op | source)
XLA Modules:
  0.0 386.4 jit_solution(17145229469995498075)
XLA Ops:
  0.6 0.0 copy-start
  0.6 3.2 multiply_reduce_fusion
  3.9 0.1 broadcast_in_dim.2
  4.0 0.1 copy-done
  4.1 4.5 %fusion = f32[512,512]{1,0:T(8,128)S(1)} fusion(bf16[512,4096]{1,0:T(8,128)(2,1)S(1)} %copy-done, bf16[4096,512]{1,0:T(8,128)(2,1)} %param.3), kind=kOutput, calls=%fused_computation.3 | convolution fusion | flops 2147483648 | bytes 9437184 | tf_op jit(solution)/shard_map/dot_general | solution.py:383
  8.6 0.1 pad_maximum_fusion.local_ref
  8.7 22.9 %shard_map.41 = (f32[128,640]{1,0:T(8,128)S(1)}, bf16[512,512]{1,0:T(8,128)(2,1)S(1)}) custom-call(f32[512,640]{1,0:T(8,128)S(1)} %pad_maximum_fusion.local_ref), custom_call_target="tpu_custom_call" | custom-call | tf_op jit(solution)/shard_map/pallas_call | solution.py:128
  31.6 118.4 %shard_map.42.both_ref = f32[1024,512]{1,0:T(8,128)S(1)} custom-call(bf16[512,512]{1,0:T(8,128)(2,1)S(1)} %get-tuple-element.4.weighted_ref, bf16[512,4096]{1,0:T(8,128)(2,1)S(1)} %copy-done), custom_call_target="tpu_custom_call" | custom-call | tf_op jit(solution)/shard_map/pallas_call | solution.py:355
  150.0 53.6 %shard_map.43.weighted_ref = bf16[512,512]{1,0:T(8,128)(2,1)S(1)} custom-call(f32[1024,512]{1,0:T(8,128)S(1)} %shard_map.42.both_ref, f32[128,640]{1,0:T(8,128)S(1)} %get-tuple-element.5.own_ref), custom_call_target="tpu_custom_call" | custom-call | tf_op jit(solution)/shard_map/pallas_call | solution.py:211
  203.6 119.1 %shard_map.44.both_ref = f32[1024,512]{1,0:T(8,128)S(1)} custom-call(bf16[512,512]{1,0:T(8,128)(2,1)S(1)} %shard_map.43.weighted_ref, bf16[512,4096]{1,0:T(8,128)(2,1)S(1)} %copy-done), custom_call_target="tpu_custom_call" | custom-call | tf_op jit(solution)/shard_map/pallas_call | solution.py:355
  322.7 61.8 %shard_map.45 = f32[512,640]{1,0:T(8,128)S(1)} custom-call(f32[1024,512]{1,0:T(8,128)S(1)} %shard_map.44.both_ref, f32[128,640]{1,0:T(8,128)S(1)} %get-tuple-element.5.own_ref), custom_call_target="tpu_custom_call" | custom-call | tf_op jit(solution)/shard_map/pallas_call | solution.py:211
  384.6 0.7 slice_reduce_fusion
  385.3 1.1 slice.6
Async XLA Ops:
  0.6 3.5 copy-start
